TPU v7x, 256 devices: a whole 4x4x8 slice. The times are simulated.
256 devices in a mesh: rows: 64 (over x_hi, y, z), grp: 4 (over x_lo, core).
Axes of the slice: x: 4 (x_hi: 2, x_lo: 2; x = x_hi * 2 + x_lo), y: 4, z: 8, core: 2. Of those that a mesh axis runs over, the one named last changes fastest.
Arguments:
- table: float32 [524288, 256], P(('rows', 'grp')), may hold values from -1.5 to 1.5
- hot_slot: int32 [4096], P(('rows', 'grp')), may hold values from 0 to 2047, as said below
- cold_row: int32 [256, 256, 8], P(('rows', 'grp')), may hold values from 0 to 2047, as said below
- cold_bag: int32 [256, 256, 8], P(('rows', 'grp')), may hold values from 0 to 511
- hot_pick: int32 [65536, 8], P(('rows', 'grp')), may hold values from 0 to 4095
- dense: float32 [65536, 256], P(('rows', 'grp')), may hold values from -6 to 6
- label: int32 [65536], P(('rows', 'grp')), may hold values 0 or 1
Outputs:
- pooled: float32 [65536, 256], P(('rows', 'grp'))
- new_table: float32 [524288, 256], P(('rows', 'grp'))
- hot_new: float32 [4096, 256], replicated
Inputs may be any that keep to these rules, and one draw needn't show every extreme that they name: `hot_slot`: distinct within each device's block of 16 entries; hot row h lies in the shard of device h // 16. `cold_row`: a cold slot never names a hot row of its owner. `cold_bag`: a value of 256 or more marks an empty slot.
All inputs are finite; a program needn't handle non-finite values. No bound on the sum of `label` on one device may be relied on, other than what follows from the above.
Results may differ from a plain program's by a relative error of at most 0.0029.
Values may be sent and summed in bfloat16 or wider, within the bound.
A program may use at most 64 MiB of HBM per device.

v0:
```python
import jax
import jax.numpy as jnp
from jax import lax
from jax.sharding import PartitionSpec as P


def split_up(value, dim, peers):
    shape = value.shape
    blocks = value.reshape(*shape[:dim], peers, shape[dim] // peers, *shape[dim + 1 :])
    return jnp.moveaxis(blocks, dim, 0)


def laid_out(blocks, dim):
    blocks = jnp.moveaxis(blocks, 0, dim)
    shape = blocks.shape
    return blocks.reshape(*shape[:dim], shape[dim] * shape[dim + 1], *shape[dim + 2 :])


def exchange_both(value, axis, axes, splits, concats):
    sizes = [lax.axis_size(a) for a in axes]
    blocks = split_up(value, splits[0], sizes[0])
    blocks = jnp.moveaxis(split_up(blocks, splits[1] + 1, sizes[1]), 0, 1)
    inside = blocks.shape[2:]
    blocks = blocks.reshape(-1, *inside)
    blocks = lax.all_to_all(blocks, axis, split_axis=0, concat_axis=0, tiled=True)
    blocks = laid_out(blocks.reshape(*sizes, *inside), concats[0] + 1)
    return laid_out(blocks, concats[1])


def body(table, hot_slot, cold_row, cold_bag, hot_pick, dense, label):
    n_rows = lax.axis_size("rows")
    n_grp = lax.axis_size("grp")
    width = table.shape[1]
    samples = dense.shape[0]
    own_hot = hot_slot.shape[0]
    slots = cold_row.shape[1] * cold_row.shape[2]
    per_peer = cold_row.shape[2]
    rounded = table.astype(jnp.bfloat16)
    hot_full = lax.all_gather(table[hot_slot], ("rows", "grp"), axis=0, tiled=True)
    hot_copy = hot_full.astype(jnp.bfloat16)
    requests = cold_row[0].reshape(n_rows, n_grp, per_peer)
    arrived = exchange_both(requests, ("rows", "grp"), ("rows", "grp"), (0, 1), (0, 1))
    looked = rounded[arrived.reshape(-1)].reshape(n_rows, n_grp, per_peer, width)
    returned = lax.all_to_all(
        lax.all_to_all(looked, "rows", split_axis=0, concat_axis=0, tiled=True),
        "grp",
        split_axis=1,
        concat_axis=1,
        tiled=True,
    )
    flat_rows = returned.reshape(slots, width)
    bags = cold_bag[0].reshape(slots)
    selector = jnp.arange(samples, dtype=jnp.int32)[:, None] == bags[None, :]
    cold_pooled = jnp.dot(
        selector.astype(jnp.bfloat16), flat_rows, preferred_element_type=jnp.float32
    )
    hot_pooled = jnp.sum(hot_copy[hot_pick].astype(jnp.float32), axis=1)
    pooled = cold_pooled + hot_pooled
    score = jnp.sum(pooled * dense, axis=1) / width**0.5
    err = jax.nn.sigmoid(score) - label.astype(jnp.float32)
    grad = err[:, None] * dense
    slot_grad = lax.dot_general(
        selector.astype(jnp.float32),
        grad,
        (((0,), (0,)), ((), ())),
        precision=lax.Precision.HIGHEST,
        preferred_element_type=jnp.float32,
    )
    delivered = exchange_both(
        slot_grad.reshape(n_rows, n_grp, per_peer, width),
        ("rows", "grp"),
        ("rows", "grp"),
        (0, 1),
        (0, 1),
    )
    table_grad = jax.ops.segment_sum(
        delivered.reshape(slots, width), arrived.reshape(slots), num_segments=table.shape[0]
    )
    hot_total = hot_copy.shape[0]
    spread = jnp.repeat(grad, hot_pick.shape[1], axis=0)
    hot_local = jax.ops.segment_sum(spread, hot_pick.reshape(-1), num_segments=hot_total)
    summed = lax.psum(hot_local, ("rows", "grp"))
    start = lax.axis_index(("rows", "grp")) * own_hot
    own_grad = lax.dynamic_slice_in_dim(summed, start, own_hot, 0)
    table_grad = table_grad.at[hot_slot].add(own_grad)
    new_table = table - 0.1 * table_grad
    hot_new = hot_full - 0.1 * summed
    return (pooled, new_table, hot_new)


def solution(mesh):
    placed = (
        P(("rows", "grp"), None),
        P(("rows", "grp")),
        P(("rows", "grp"), None, None),
        P(("rows", "grp"), None, None),
        P(("rows", "grp"), None),
        P(("rows", "grp"), None),
        P(("rows", "grp")),
    )
    return jax.shard_map(
        body,
        mesh=mesh,
        in_specs=placed,
        out_specs=(P(("rows", "grp"), None), P(("rows", "grp"), None), P()),
        check_vma=False,
    )
```

profile of v0, /device:TPU:1, one launch (start us, length us, event | category | flops | bytes accessed | tf_op | source)
XLA Modules:
  0.0 782.2 jit_solution(3402326476514333365)
XLA Ops:
  7.2 0.0 all-gather.3.cloned.1.call-start
  7.2 0.7 compare_select_fusion.2
  7.9 0.5 copy-done.6
  8.4 2.8 gather_fusion.1
  11.2 0.0 all-gather.3.cloned.1.call-update
  11.2 1.5 copy.38
  12.7 15.6 %all-to-all-start = ((s32[256,1,1,8]{3,2,1,0:T(1,128)}), s32[256,1,1,8]{3,2,1,0:T(1,128)S(1)}, u32[]{:S(2)}, u32[]{:S(2)}) async-start(s32[256,1,1,8]{3,2,1,0:T(1,128)} %bitcast), calls=%async_computation | async-start | bytes 262144 | tf_op jit(solution)/shard_map/all_to_all | solution.py:25
  28.3 1.7 convert_element_type.14
  30.0 11.0 %all-to-all-done = s32[256,1,1,8]{3,2,1,0:T(1,128)S(1)} async-done(((s32[256,1,1,8]{3,2,1,0:T(1,128)}), s32[256,1,1,8]{3,2,1,0:T(1,128)S(1)}, u32[]{:S(2)}, u32[]{:S(2)}) %all-to-all-start) | async-done | bytes 8224 | tf_op jit(solution)/shard_map/all_to_all | solution.py:25
  41.1 0.2 reshape_reshape.6
  41.3 7.5 gather_fusion
  48.8 32.7 %all_to_all.20 = bf16[64,4,8,256]{3,2,1,0:T(8,128)(2,1)S(1)} all-to-all(bf16[64,4,8,256]{3,2,1,0:T(8,128)(2,1)S(1)} %bitcast.38), channel_id=1, replica_groups=mesh['rows'=64,'grp'=4] {'rows'}, dimensions={0} | all-to-all | bytes 2097152 | tf_op jit(solution)/shard_map/all_to_all | solution.py:45
  81.4 1.0 copy.39
  82.5 5.8 all-to-all-start.2
  88.3 0.0 copy-done.1
  88.3 0.8 copy.43
  89.1 0.0 copy-done.2
  89.1 0.1 copy.41
  89.3 0.1 reshape.82
  89.4 0.0 copy-done.4
  89.4 0.1 copy.37
  89.5 0.1 eq.16
  89.7 12.9 %all-to-all-done.2 = bf16[64,4,8,256]{3,2,0,1:T(8,128)(2,1)S(1)} async-done(((bf16[64,4,8,256]{3,2,0,1:T(8,128)(2,1)}), bf16[64,4,8,256]{3,2,0,1:T(8,128)(2,1)S(1)}, u32[]{:S(2)}, u32[]{:S(2)}) %all-to-all-start.2) | async-done | bytes 1048608 | tf_op jit(solution)/shard_map/all_to_all | solution.py:44
  102.6 1.1 copy.40
  103.7 329.3 %all-gather.3.cloned.1.call-done = f32[4096,256]{1,0:T(8,128)} async-done(((f32[16,256]{1,0:T(8,128)}), f32[4096,256]{1,0:T(8,128)}) %all-gather.3.cloned.1.call-update) | async-done | bytes 4194320 | tf_op jit(solution)/shard_map/all_gather | solution.py:39
  433.0 2.4 convert_element_type.15
  435.4 7.5 gather_fusion.2
  442.9 0.0 copy-start.5
  442.9 0.7 convert_reduce_fusion
  443.6 0.1 copy.42
  443.7 2.0 multiply_reduce_fusion
  445.7 0.0 copy-done.5
  445.8 0.1 broadcast_multiply_fusion
  445.9 3.2 fusion.7
  449.0 9.4 %all-to-all-start.3 = ((f32[256,1,1,8,256]{4,3,2,1,0:T(8,128)}), f32[256,1,1,8,256]{4,3,2,1,0:T(8,128)S(1)}, u32[]{:S(2)}, u32[]{:S(2)}) async-start(f32[256,1,1,8,256]{4,3,2,1,0:T(8,128)} %fusion.7), calls=%async_computation.3 | async-start | bytes 4194304 | tf_op jit(solution)/shard_map/all_to_all | solution.py:25
  458.5 0.2 all-reduce.2.cloned.1.call-start
  458.7 0.1 copy.45
  458.8 0.1 reshape.98
  459.0 13.8 %scatter_custom_fusion.1 = f32[4096,256]{1,0:T(8,128)} fusion(s32[2048]{0:T(1024)S(1)} %reshape.98, f32[]{:T(128)} %constant.15.clone.1, f32[256,256]{1,0:T(8,128)S(1)} %broadcast_multiply_fusion), kind=kCustom, calls=%fused_computation.10 | custom fusion | flops 524288 | bytes 4456452 | tf_op jit(solution)/shard_map/scatter-add | solution.py:81
  472.8 0.0 all-reduce.2.cloned.1.call-update
  472.8 0.2 reshape.90
  473.0 0.8 copy.46
  473.8 275.5 %all-reduce.2.cloned.1.call-done = f32[4096,256]{1,0:T(8,128)} async-done(((f32[4096,256]{1,0:T(8,128)}), f32[4096,256]{1,0:T(8,128)}) %all-reduce.2.cloned.1.call-update) | async-done | bytes 4194320 | tf_op jit(solution)/shard_map/psum | solution.py:82
  749.3 6.0 multiply_subtract_fusion
  755.3 0.0 all-to-all-done.3
  755.3 13.0 %scatter_custom_fusion = f32[2048,256]{1,0:T(8,128)} fusion(s32[2048]{0:T(1024)S(1)} %reshape.90, f32[256,1,1,8,256]{4,3,2,1,0:T(8,128)S(1)} %all-to-all-done.3, f32[]{:T(128)} %constant.15.clone.1), kind=kCustom, calls=%fused_computation.7 | custom fusion | flops 524288 | bytes 4194308 | tf_op jit(solution)/shard_map/scatter-add | solution.py:76
  768.4 3.9 scatter_custom_fusion.2
  772.2 3.2 multiply_subtract_fusion.1
  (14 shorter events, 0.1 us)
Async XLA Ops:
  7.2 425.8 %all-gather.3.cloned.1.call-start = ((), (), s32[]{:S(2)}) async-start(), calls=%async_computation.5 | async-start | bytes 4210688 | tf_op jit(solution)/shard_map/all_gather | solution.py:39
  7.9 0.5 copy-start.6
  12.7 28.4 %all-to-all-start = ((s32[256,1,1,8]{3,2,1,0:T(1,128)}), s32[256,1,1,8]{3,2,1,0:T(1,128)S(1)}, u32[]{:S(2)}, u32[]{:S(2)}) async-start(s32[256,1,1,8]{3,2,1,0:T(1,128)} %bitcast), calls=%async_computation | async-start | bytes 262144 | tf_op jit(solution)/shard_map/all_to_all | solution.py:25
  81.4 6.9 copy-start.1
  81.4 7.7 copy-start.2
  81.4 8.0 %copy-start.4 = (s32[1,256,8]{1,2,0:T(8,128)S(1)}, s32[1,256,8]{1,2,0:T(8,128)}, u32[]{:S(2)}) copy-start(s32[1,256,8]{1,2,0:T(8,128)} %param.10) | copy-start | bytes 24580
  82.5 20.1 %all-to-all-start.2 = ((bf16[64,4,8,256]{3,2,0,1:T(8,128)(2,1)}), bf16[64,4,8,256]{3,2,0,1:T(8,128)(2,1)S(1)}, u32[]{:S(2)}, u32[]{:S(2)}) async-start(bf16[64,4,8,256]{3,2,0,1:T(8,128)(2,1)} %copy.39), calls=%async_computation.2 | async-start | bytes 2097152 | tf_op jit(solution)/shard_map/all_to_all | solution.py:44
  442.9 2.8 copy-start.5
  449.0 9.7 %copy-start.3 = (s32[256,8]{0,1:T(8,128)S(1)}, s32[256,8]{0,1:T(8,128)}, u32[]{:S(2)}) copy-start(s32[256,8]{0,1:T(8,128)} %param.11) | copy-start | bytes 24580
  449.0 306.3 %all-to-all-start.3 = ((f32[256,1,1,8,256]{4,3,2,1,0:T(8,128)}), f32[256,1,1,8,256]{4,3,2,1,0:T(8,128)S(1)}, u32[]{:S(2)}, u32[]{:S(2)}) async-start(f32[256,1,1,8,256]{4,3,2,1,0:T(8,128)} %fusion.7), calls=%async_computation.3 | async-start | bytes 4194304 | tf_op jit(solution)/shard_map/all_to_all | solution.py:25
  458.5 290.8 %all-reduce.2.cloned.1.call-start = ((), (), s32[]{:S(2)}) async-start(), calls=%async_computation.4 | async-start | bytes 8388608 | tf_op jit(solution)/shard_map/psum | solution.py:82
  768.4 3.9 copy-start
Sparse Core Ops, SparseCore 0:
  11.3 421.6 all-gather.2
  472.9 276.3 all-reduce.1
where the time goes:
time: 784 us; the launch traced here: 782 us
  waiting for transfers between devices  629 us (80%)
  other arithmetic  45.5 us (6%)
  blocking collectives  32.7 us (4%)
  starting transfers between devices  31.2 us (4%)
  local copies, waits for them, and re-layouts  24.8 us (3%)
  between operations  14.2 us (2%)
    all_gather x1, waiting for transfers between devices, body(): lax.all_gather(table[hot_slot], ('rows', 'grp'), axis=0, tiled=True)  329 us
    psum x1, waiting for transfers between devices, body(): summed = lax.psum(hot_local, ('rows', 'grp'))  275 us
    all_to_all x1, blocking collectives, body(): lax.all_to_all(looked, 'rows', split_axis=0, concat_axis=0, tiled=True)  32.7 us
    all_to_all x2, starting transfers between devices, exchange_both(): lax.all_to_all(blocks, axis, split_axis=0, concat_axis=0, tiled=True)  25.1 us
  transfers between devices with their start and end apart: 5, of which 4 were waited for; matrix products, arithmetic and copies ran while one was open for 5% of the time, Pallas kernels for 0%

commit v1 on v0

v1 whole, which is shorter than its diff:
```python
import jax
import jax.numpy as jnp
from jax import lax
from jax.sharding import PartitionSpec as P

AXES = ("rows", "grp")


def exchange(blocks):
    return lax.all_to_all(blocks, AXES, split_axis=0, concat_axis=0, tiled=True)


def split_bf16(value):
    high = lax.reduce_precision(value, exponent_bits=8, mantissa_bits=7)
    return high.astype(jnp.bfloat16), (value - high).astype(jnp.bfloat16)


def body(table, hot_slot, cold_row, cold_bag, hot_pick, dense, label):
    n = lax.axis_size("rows") * lax.axis_size("grp")
    n_table, width = table.shape
    samples = dense.shape[0]
    own_hot = hot_slot.shape[0]
    cap = cold_row.shape[2]
    slots = cold_row.shape[1] * cap
    f32, bf16 = jnp.float32, jnp.bfloat16
    rounded = table.astype(bf16)

    arrived = exchange(cold_row[0]).reshape(slots)
    hot_old = table[hot_slot]
    hot_copy = exchange(jnp.broadcast_to(hot_old.astype(bf16)[None], (n, own_hot, width)))
    hot_copy = hot_copy.reshape(n * own_hot, width)

    row_ids = jnp.arange(n_table, dtype=jnp.int32)
    at_row = (arrived[:, None] == row_ids[None, :]).astype(bf16)
    looked = jnp.dot(at_row, rounded, preferred_element_type=f32).astype(bf16)
    returned = exchange(looked.reshape(n, cap, width)).reshape(slots, width)

    bags = cold_bag[0].reshape(slots)
    sample_ids = jnp.arange(samples, dtype=jnp.int32)
    selector = (sample_ids[:, None] == bags[None, :]).astype(bf16)
    hot_ids = jnp.arange(n * own_hot, dtype=jnp.int32)
    counts = sum(
        (hot_pick[:, j][:, None] == hot_ids[None, :]).astype(f32)
        for j in range(hot_pick.shape[1])
    ).astype(bf16)
    pooled = jnp.dot(selector, returned, preferred_element_type=f32)
    pooled = pooled + jnp.dot(counts, hot_copy, preferred_element_type=f32)
    score = jnp.sum(pooled * dense, axis=1) / width**0.5
    err = jax.nn.sigmoid(score) - label.astype(f32)
    grad = err[:, None] * dense
    high, low = split_bf16(grad)

    first = (((0,), (0,)), ((), ()))
    slot_grad = lax.dot_general(selector, high, first, preferred_element_type=f32).astype(bf16)
    delivered = exchange(slot_grad.reshape(n, cap, width)).reshape(slots, width)

    hot_local = lax.dot_general(counts, high, first, preferred_element_type=f32)
    hot_local = hot_local + lax.dot_general(counts, low, first, preferred_element_type=f32)
    parts = exchange(hot_local.astype(bf16).reshape(n, own_hot, width))
    own_grad = jnp.sum(parts.astype(f32), axis=0)
    hot_own_new = hot_old - 0.1 * own_grad
    hot_new = exchange(jnp.broadcast_to(hot_own_new.astype(bf16)[None], (n, own_hot, width)))
    hot_new = hot_new.reshape(n * own_hot, width).astype(f32)

    table_grad = lax.dot_general(at_row, delivered, first, preferred_element_type=f32)
    at_hot = (row_ids[:, None] == hot_slot[None, :]).astype(f32)
    table_grad = table_grad + jnp.dot(
        at_hot, own_grad, precision=lax.Precision.HIGHEST, preferred_element_type=f32
    )
    new_table = table - 0.1 * table_grad
    return (pooled, new_table, hot_new)


def solution(mesh):
    placed = (
        P(AXES, None),
        P(AXES),
        P(AXES, None, None),
        P(AXES, None, None),
        P(AXES, None),
        P(AXES, None),
        P(AXES),
    )
    return jax.shard_map(
        body,
        mesh=mesh,
        in_specs=placed,
        out_specs=(P(AXES, None), P(AXES, None), P()),
        check_vma=False,
    )
```

time: 784 us -> 300 us (0.38)
  waiting for transfers between devices: 629 us -> 204 us
  other arithmetic: 45.5 us -> 4.46 us
  blocking collectives: 32.7 us -> 0 us
  matrix products: 5.14 us -> 31.1 us
  starting transfers between devices: 31.2 us -> 50.8 us
  local copies, waits for them, and re-layouts: 24.8 us -> 8.57 us
  between operations: 14.2 us -> 0.86 us
    all_gather x1 -> x0, waiting for transfers between devices: 329 us -> none  [body(): lax.all_gather(table[hot_slot], ('rows', 'grp'), axis=0, tiled=True)]
    psum x1 -> x0, waiting for transfers between devices: 275 us -> none  [body(): summed = lax.psum(hot_local, ('rows', 'grp'))]
    all_to_all x3 -> x6, waiting for transfers between devices: 24 us -> 204 us  [exchange(): return lax.all_to_all(blocks, AXES, split_axis=0, concat_axis=0, tiled=True)]
    all_to_all x1 -> x0, blocking collectives: 32.7 us -> none  [body(): lax.all_to_all(looked, 'rows', split_axis=0, concat_axis=0, tiled=True)]
    scatter-add x3 -> x0, other arithmetic: 30.7 us -> none  [the longest x1 13.8 us: body(): jax.ops.segment_sum(spread, hot_pick.reshape(-1), num_segments=hot_total)]
    dot_general x2 -> x8, matrix products: 5.14 us -> 31.1 us  [the longest x1 6.44 us: body(): pooled = pooled + jnp.dot(counts, hot_copy, preferred_element_type=f32)]
    all_to_all x3 -> x6, starting transfers between devices: 30.9 us -> 50.8 us  [exchange(): return lax.all_to_all(blocks, AXES, split_axis=0, concat_axis=0, tiled=True)]
    gather x3 -> x1, local copies, waits for them, and re-layouts: 17.8 us -> 2.16 us  [body(): hot_old = table[hot_slot]]
  transfers between devices with their start and end apart: 5 -> 6, of which waited for: 4 -> 6; matrix products, arithmetic and copies ran while one was open for 5% -> 8% of each run, Pallas kernels for 0% -> 0%
where the time goes in v1:
time: 300 us; the launch traced here: 299 us
  waiting for transfers between devices  204 us (68%)
  starting transfers between devices  50.8 us (17%)
  matrix products  31.1 us (10%)
  local copies, waits for them, and re-layouts  8.57 us (3%)
  other arithmetic  4.46 us (1%)
    all_to_all x6, waiting for transfers between devices, exchange(): return lax.all_to_all(blocks, AXES, split_axis=0, concat_axis=0, tiled=True)  204 us
    all_to_all x6, starting transfers between devices, exchange(): return lax.all_to_all(blocks, AXES, split_axis=0, concat_axis=0, tiled=True)  50.8 us
    dot_general x1, matrix products, body(): pooled = pooled + jnp.dot(counts, hot_copy, preferred_element_type=f32)  6.44 us
    dot_general x1, matrix products, body(): lax.dot_general(counts, low, first, preferred_element_type=f32)  6.34 us
  transfers between devices with their start and end apart: 6, of which 6 were waited for; matrix products, arithmetic and copies ran while one was open for 8% of the time, Pallas kernels for 0%

profile of v1, /device:TPU:1, one launch (start us, length us, event | category | flops | bytes accessed | tf_op | source)
XLA Modules:
  0.0 299.4 jit_solution(16601904762801705510)
XLA Ops:
  0.6 0.0 copy-start
  0.6 1.6 copy.17
  2.3 15.6 %all-to-all-start = ((s32[256,1,8]{2,1,0:T(1,128)}), s32[256,1,8]{2,1,0:T(1,128)S(1)}, u32[]{:S(2)}, u32[]{:S(2)}) async-start(s32[256,1,8]{2,1,0:T(1,128)} %bitcast), calls=%async_computation | async-start | bytes 262144 | tf_op jit(solution)/shard_map/all_to_all | solution.py:10
  17.9 0.7 compare_select_fusion
  18.6 2.2 gather_fusion
  20.8 9.9 %all-to-all-done = s32[256,1,8]{2,1,0:T(1,128)S(1)} async-done(((s32[256,1,8]{2,1,0:T(1,128)}), s32[256,1,8]{2,1,0:T(1,128)S(1)}, u32[]{:S(2)}, u32[]{:S(2)}) %all-to-all-start) | async-done | bytes 8224 | tf_op jit(solution)/shard_map/all_to_all | solution.py:10
  30.7 1.5 broadcast_in_dim.7
  32.1 7.6 %all-to-all-start.2 = ((bf16[256,16,256]{2,1,0:T(8,128)(2,1)}), bf16[256,16,256]{2,1,0:T(8,128)(2,1)}, u32[]{:S(2)}, u32[]{:S(2)}) async-start(bf16[256,16,256]{2,1,0:T(8,128)(2,1)} %broadcast_in_dim.7), calls=%async_computation.2 | async-start | bytes 4194304 | tf_op jit(solution)/shard_map/all_to_all | solution.py:10
  39.8 0.5 broadcast.29
  40.3 1.0 reduce.3
  41.2 0.1 eq.167
  41.4 0.0 copy-done
  41.4 0.0 copy-start.3
  41.4 0.0 copy-start.2
  41.4 0.0 copy-start.4
  41.4 4.0 %fusion.10 = bf16[256,8,256]{2,1,0:T(8,128)(2,1)} fusion(s32[2048]{0:T(1024)S(1)} %eq.167, f32[2048,256]{1,0:T(8,128)S(1)} %copy-done), kind=kOutput, calls=%fused_computation.27 | convolution fusion | flops 2152726528 | bytes 3153920 | tf_op jit(solution)/shard_map/dot_general | solution.py:35
  45.4 45.6 %all-to-all-done.2 = bf16[256,16,256]{2,1,0:T(8,128)(2,1)} async-done(((bf16[256,16,256]{2,1,0:T(8,128)(2,1)}), bf16[256,16,256]{2,1,0:T(8,128)(2,1)}, u32[]{:S(2)}, u32[]{:S(2)}) %all-to-all-start.2) | async-done | bytes 2097184 | tf_op jit(solution)/shard_map/all_to_all | solution.py:10
  91.0 7.6 %all-to-all-start.1 = ((bf16[256,8,256]{2,1,0:T(8,128)(2,1)}), bf16[256,8,256]{2,1,0:T(8,128)(2,1)S(1)}, u32[]{:S(2)}, u32[]{:S(2)}) async-start(bf16[256,8,256]{2,1,0:T(8,128)(2,1)} %fusion.10), calls=%async_computation.1 | async-start | bytes 2097152 | tf_op jit(solution)/shard_map/all_to_all | solution.py:10
  98.6 0.0 copy-done.3
  98.6 0.1 copy.16
  98.7 0.1 eq.164
  98.9 0.0 copy-done.2
  98.9 0.1 copy.18
  99.0 0.0 copy-done.4
  99.0 0.0 copy-start.5
  99.0 6.4 %fusion.22 = f32[256,256]{0,1:T(8,128)S(1)} fusion(bf16[4096,256]{1,0:T(8,128)(2,1)} %bitcast.11, s32[256]{0:T(256)S(1)} %bitcast.47, s32[256]{0:T(256)S(1)} %bitcast.50, s32[256]{0:T(256)S(1)} %bitcast.32, s32[256]{0:T(256)S(1)} %bitcast.35, s32[256]{0:T(256)S(1)} %bitcast.38, s32[256]{0:T(256)S(1)} %bitcast.41, s32[256]{0:T(256)S(1)} %bitcast.44, ...), kind=kOutput, calls=%fused_computation.46 | convolution fusion | flops 562036736 | bytes 2367488 | tf_op jit(solution)/shard_map/dot_general | solution.py:47
  105.5 23.6 %all-to-all-done.1 = bf16[256,8,256]{2,1,0:T(8,128)(2,1)S(1)} async-done(((bf16[256,8,256]{2,1,0:T(8,128)(2,1)}), bf16[256,8,256]{2,1,0:T(8,128)(2,1)S(1)}, u32[]{:S(2)}, u32[]{:S(2)}) %all-to-all-start.1) | async-done | bytes 1048608 | tf_op jit(solution)/shard_map/all_to_all | solution.py:10
  129.1 0.7 multiply_reduce_fusion
  129.8 0.0 copy-done.5
  129.8 4.6 %fusion.21 = f32[4096,256]{1,0:T(8,128)S(1)} fusion(f32[256,256]{1,0:T(8,128)S(1)} %copy-done.2, f32[256]{0:T(256)S(1)} %divide_subtract_fusion, s32[256]{0:T(256)S(1)} %bitcast.48, s32[256]{0:T(256)S(1)} %bitcast.51, s32[256]{0:T(256)S(1)} %bitcast.33, s32[256]{0:T(256)S(1)} %bitcast.36, s32[256]{0:T(256)S(1)} %bitcast.39, s32[256]{0:T(256)S(1)} %bitcast.42, ...), kind=kOutput, calls=%fused_computation.45 | convolution fusion | flops 562233344 | bytes 4465664 | tf_op jit(solution)/shard_map/dot_general | solution.py:57
  134.4 6.3 %fusion.4 = bf16[4096,256]{1,0:T(8,128)(2,1)} fusion(f32[4096,256]{1,0:T(8,128)S(1)} %fusion.21, f32[256,256]{1,0:T(8,128)S(1)} %copy-done.2, f32[256]{0:T(256)S(1)} %divide_subtract_fusion, s32[256]{0:T(256)S(1)} %bitcast.49, s32[256]{0:T(256)S(1)} %bitcast.52, s32[256]{0:T(256)S(1)} %bitcast.34, s32[256]{0:T(256)S(1)} %bitcast.37, s32[256]{0:T(256)S(1)} %bitcast.40, ...), kind=kOutput, calls=%fused_computation.7 | convolution fusion | flops 564396032 | bytes 6562816 | tf_op jit(solution)/shard_map/dot_general | solution.py:58
  140.8 6.3 %all-to-all-start.4 = ((bf16[256,16,256]{2,1,0:T(8,128)(2,1)}), bf16[256,16,256]{2,1,0:T(8,128)(2,1)S(1)}, u32[]{:S(2)}, u32[]{:S(2)}) async-start(bf16[256,16,256]{2,1,0:T(8,128)(2,1)} %bitcast.28), calls=%async_computation.4 | async-start | bytes 4194304 | tf_op jit(solution)/shard_map/all_to_all | solution.py:10
  147.1 1.8 fusion.9
  148.8 50.3 %all-to-all-done.4 = bf16[256,16,256]{2,1,0:T(8,128)(2,1)S(1)} async-done(((bf16[256,16,256]{2,1,0:T(8,128)(2,1)}), bf16[256,16,256]{2,1,0:T(8,128)(2,1)S(1)}, u32[]{:S(2)}, u32[]{:S(2)}) %all-to-all-start.4) | async-done | bytes 2097184 | tf_op jit(solution)/shard_map/all_to_all | solution.py:10
  199.1 7.4 %all-to-all-start.3 = ((bf16[256,8,256]{2,1,0:T(8,128)(2,1)}), bf16[256,8,256]{2,1,0:T(8,128)(2,1)S(1)}, u32[]{:S(2)}, u32[]{:S(2)}) async-start(bf16[256,8,256]{2,1,0:T(8,128)(2,1)} %fusion.9), calls=%async_computation.3 | async-start | bytes 2097152 | tf_op jit(solution)/shard_map/all_to_all | solution.py:10
  206.5 0.3 convert_reduce_fusion
  206.8 30.3 %all-to-all-done.3 = bf16[256,8,256]{2,1,0:T(8,128)(2,1)S(1)} async-done(((bf16[256,8,256]{2,1,0:T(8,128)(2,1)}), bf16[256,8,256]{2,1,0:T(8,128)(2,1)S(1)}, u32[]{:S(2)}, u32[]{:S(2)}) %all-to-all-start.3) | async-done | bytes 1048608 | tf_op jit(solution)/shard_map/all_to_all | solution.py:10
  237.1 1.5 broadcast_in_dim.8
  238.6 6.3 %all-to-all-start.5 = ((bf16[256,16,256]{2,1,0:T(8,128)(2,1)}), bf16[256,16,256]{2,1,0:T(8,128)(2,1)S(1)}, u32[]{:S(2)}, u32[]{:S(2)}) async-start(bf16[256,16,256]{2,1,0:T(8,128)(2,1)} %broadcast_in_dim.8), calls=%async_computation.5 | async-start | bytes 4194304 | tf_op jit(solution)/shard_map/all_to_all | solution.py:10
  244.9 0.8 copy.19
  245.7 0.0 copy-start.1
  245.7 0.0 copy-start.6
  245.7 4.9 %fusion = f32[2048,256]{1,0:T(8,128)S(1)} fusion(s32[2048]{0:T(1024)S(1)} %eq.167, bf16[256,8,256]{2,1,0:T(8,128)(2,1)S(1)} %all-to-all-done.3), kind=kOutput, calls=%fused_computation.2 | convolution fusion | flops 2151677952 | bytes 3153920 | tf_op jit(solution)/shard_map/dot_general | solution.py:65
  250.7 0.0 copy-done.1
  250.7 0.0 copy-done.6
  250.7 2.3 fusion.6
  253.0 43.9 %all-to-all-done.5 = bf16[256,16,256]{2,1,0:T(8,128)(2,1)S(1)} async-done(((bf16[256,16,256]{2,1,0:T(8,128)(2,1)}), bf16[256,16,256]{2,1,0:T(8,128)(2,1)S(1)}, u32[]{:S(2)}, u32[]{:S(2)}) %all-to-all-start.5) | async-done | bytes 2097184 | tf_op jit(solution)/shard_map/all_to_all | solution.py:10
  296.9 2.5 bitcast_convert_fusion
  (5 shorter events, 0.0 us)
Async XLA Ops:
  0.6 40.7 %copy-start = (f32[2048,256]{1,0:T(8,128)S(1)}, f32[2048,256]{1,0:T(8,128)}, u32[]{:S(2)}) copy-start(f32[2048,256]{1,0:T(8,128)} %param.7) | copy-start | bytes 6291460
  2.3 28.4 %all-to-all-start = ((s32[256,1,8]{2,1,0:T(1,128)}), s32[256,1,8]{2,1,0:T(1,128)S(1)}, u32[]{:S(2)}, u32[]{:S(2)}) async-start(s32[256,1,8]{2,1,0:T(1,128)} %bitcast), calls=%async_computation | async-start | bytes 262144 | tf_op jit(solution)/shard_map/all_to_all | solution.py:10
  32.1 58.9 %all-to-all-start.2 = ((bf16[256,16,256]{2,1,0:T(8,128)(2,1)}), bf16[256,16,256]{2,1,0:T(8,128)(2,1)}, u32[]{:S(2)}, u32[]{:S(2)}) async-start(bf16[256,16,256]{2,1,0:T(8,128)(2,1)} %broadcast_in_dim.7), calls=%async_computation.2 | async-start | bytes 4194304 | tf_op jit(solution)/shard_map/all_to_all | solution.py:10
  41.4 57.2 %copy-start.3 = (s32[1,256,8]{1,2,0:T(8,128)S(1)}, s32[1,256,8]{1,2,0:T(8,128)}, u32[]{:S(2)}) copy-start(s32[1,256,8]{1,2,0:T(8,128)} %param.10) | copy-start | bytes 24580
  41.4 57.5 %copy-start.2 = (f32[256,256]{1,0:T(8,128)S(1)}, f32[256,256]{1,0:T(8,128)}, u32[]{:S(2)}) copy-start(f32[256,256]{1,0:T(8,128)} %param.12) | copy-start | bytes 786436
  41.4 57.6 %copy-start.4 = (s32[256,8]{0,1:T(8,128)S(1)}, s32[256,8]{0,1:T(8,128)}, u32[]{:S(2)}) copy-start(s32[256,8]{0,1:T(8,128)} %param.11) | copy-start | bytes 24580
  91.0 38.1 %all-to-all-start.1 = ((bf16[256,8,256]{2,1,0:T(8,128)(2,1)}), bf16[256,8,256]{2,1,0:T(8,128)(2,1)S(1)}, u32[]{:S(2)}, u32[]{:S(2)}) async-start(bf16[256,8,256]{2,1,0:T(8,128)(2,1)} %fusion.10), calls=%async_computation.1 | async-start | bytes 2097152 | tf_op jit(solution)/shard_map/all_to_all | solution.py:10
  99.0 30.8 %copy-start.5 = (s32[256]{0:T(256)S(1)}, s32[256]{0:T(256)}, u32[]{:S(2)}) copy-start(s32[256]{0:T(256)} %param.13) | copy-start | bytes 3076
  140.8 58.3 %all-to-all-start.4 = ((bf16[256,16,256]{2,1,0:T(8,128)(2,1)}), bf16[256,16,256]{2,1,0:T(8,128)(2,1)S(1)}, u32[]{:S(2)}, u32[]{:S(2)}) async-start(bf16[256,16,256]{2,1,0:T(8,128)(2,1)} %bitcast.28), calls=%async_computation.4 | async-start | bytes 4194304 | tf_op jit(solution)/shard_map/all_to_all | solution.py:10
  199.1 38.1 %all-to-all-start.3 = ((bf16[256,8,256]{2,1,0:T(8,128)(2,1)}), bf16[256,8,256]{2,1,0:T(8,128)(2,1)S(1)}, u32[]{:S(2)}, u32[]{:S(2)}) async-start(bf16[256,8,256]{2,1,0:T(8,128)(2,1)} %fusion.9), calls=%async_computation.3 | async-start | bytes 2097152 | tf_op jit(solution)/shard_map/all_to_all | solution.py:10
  238.6 58.3 %all-to-all-start.5 = ((bf16[256,16,256]{2,1,0:T(8,128)(2,1)}), bf16[256,16,256]{2,1,0:T(8,128)(2,1)S(1)}, u32[]{:S(2)}, u32[]{:S(2)}) async-start(bf16[256,16,256]{2,1,0:T(8,128)(2,1)} %broadcast_in_dim.8), calls=%async_computation.5 | async-start | bytes 4194304 | tf_op jit(solution)/shard_map/all_to_all | solution.py:10
  245.7 5.0 %copy-start.1 = (f32[2048,256]{1,0:T(8,128)S(1)}, f32[2048,256]{1,0:T(8,128)}, u32[]{:S(2)}) copy-start(f32[2048,256]{1,0:T(8,128)} %param.7) | copy-start | bytes 6291460
  245.7 5.0 %copy-start.6 = (s32[16]{0:T(128)S(1)}, s32[16]{0:T(128)}, u32[]{:S(2)}) copy-start(s32[16]{0:T(128)} %param.8) | copy-start | bytes 196

commit v2 on v1

v2 whole, which is shorter than its diff:
```python
import functools
import math

import jax
import jax.numpy as jnp
from jax import lax
from jax.experimental import pallas as pl
from jax.experimental.pallas import tpu as pltpu
from jax.sharding import PartitionSpec as P

AXES = ("rows", "grp")
MESH = pl.DeviceIdType.MESH
SHAPE = (2, 4, 8, 2, 2)


def exchange(blocks):
    return lax.all_to_all(blocks, AXES, split_axis=0, concat_axis=0, tiled=True)


def split_bf16(value):
    high = lax.reduce_precision(value, exponent_bits=8, mantissa_bits=7)
    return high.astype(jnp.bfloat16), (value - high).astype(jnp.bfloat16)


class Place:
    def __init__(self, dims):
        self.dims = dims
        x_hi, y, z, x_lo, core = dims
        r, g = lax.axis_index("rows"), lax.axis_index("grp")
        self.x_hi, self.y, self.z = r // (y * z), (r // z) % y, r % z
        self.x_lo, self.c = g // core, g % core
        self.x = self.x_hi * x_lo + self.x_lo
        self.n = (x_hi * x_lo, y, z)

    def device(self, x, y, z, c):
        _, n_y, n_z, n_lo, n_core = self.dims
        return ((x // n_lo * n_y + y) * n_z + z, x % n_lo * n_core + c)

    def along_x(self, k):
        x = (self.x + k) % self.n[0]
        return x, self.device(x, self.y, self.z, self.c)

    def along_y(self, k):
        y = (self.y + k) % self.n[1]
        return y, self.device(self.x, y, self.z, self.c)

    def along_z(self, k):
        z = (self.z + k) % self.n[2]
        return z, self.device(self.x, self.y, z, self.c)

    def partner(self):
        return self.device(self.x, self.y, self.z, 1 - self.c)

    def meet(self):
        barrier = pltpu.get_barrier_semaphore()
        n_x, n_y, n_z = self.n
        peers = [self.along_z(k)[1] for k in range(1, n_z)]
        peers += [self.along_y(k)[1] for k in range(1, n_y)]
        peers += [self.along_x(k)[1] for k in range(1, n_x)]
        peers += [self.partner()]
        for peer in peers:
            pl.semaphore_signal(barrier, inc=1, device_id=peer, device_id_type=MESH)
        pl.semaphore_wait(barrier, len(peers))


def copies_of_gather(dims):
    n_x, n_y, n_z = dims[0] * dims[3], dims[1], dims[2]
    return (n_z - 1) + 2 * (n_y - 1) + 2 * (n_x - 1) + 1


def copies_of_scatter(dims):
    return copies_of_gather(dims)


class Sender:
    def __init__(self, send_sem, recv_sem):
        self.send_sem, self.recv_sem = send_sem, recv_sem
        self.used = 0
        self.all = []

    def start(self, src, dst, device):
        copy = pltpu.make_async_remote_copy(
            src_ref=src,
            dst_ref=dst,
            send_sem=self.send_sem.at[self.used],
            recv_sem=self.recv_sem.at[self.used],
            device_id=device,
            device_id_type=MESH,
        )
        copy.start()
        self.used += 1
        self.all.append(copy)
        return copy

    def finish(self):
        for copy in self.all:
            copy.wait_send()


def gather_rows(me, own, full, sender, local_sem):
    n_x, n_y, n_z = me.n
    half = n_z // 2
    mine = full.at[me.x_hi, me.y, me.z, me.x_lo, me.c]
    keep = pltpu.make_async_copy(own, mine, local_sem)
    keep.start()
    stage = [sender.start(own, mine, me.along_z(k)[1]) for k in range(1, n_z)]
    keep.wait()
    for copy in stage:
        copy.wait_recv()
    low, top = pl.ds(0, half), pl.ds(half, half)
    line = full.at[me.x_hi, me.y, low, me.x_lo, me.c]
    stage = [sender.start(line, line, me.along_y(k)[1]) for k in range(1, n_y)]
    line = full.at[me.x_hi, me.y, top, me.x_lo, me.c]
    stage += [sender.start(line, line, me.along_x(k)[1]) for k in range(1, n_x)]
    for copy in stage:
        copy.wait_recv()
    plane = full.at[me.x_hi, :, low, me.x_lo, me.c]
    stage = [sender.start(plane, plane, me.along_x(k)[1]) for k in range(1, n_x)]
    plane = full.at[:, me.y, top, :, me.c]
    stage += [sender.start(plane, plane, me.along_y(k)[1]) for k in range(1, n_y)]
    for copy in stage:
        copy.wait_recv()
    side = full.at[:, :, :, :, me.c]
    sender.start(side, side, me.partner()).wait_recv()


def gather_kernel(dims, own, full, send_sem, recv_sem, local_sem):
    me = Place(dims)
    me.meet()
    sender = Sender(send_sem, recv_sem)
    gather_rows(me, own, full, sender, local_sem)
    sender.finish()


def gather_hot(own, dims):
    count = copies_of_gather(dims)
    full = pl.pallas_call(
        functools.partial(gather_kernel, dims),
        out_shape=jax.ShapeDtypeStruct((*dims, *own.shape), own.dtype),
        in_specs=[pl.BlockSpec(memory_space=pltpu.VMEM)],
        out_specs=pl.BlockSpec(memory_space=pltpu.VMEM),
        scratch_shapes=[
            pltpu.SemaphoreType.DMA((count,)),
            pltpu.SemaphoreType.DMA((count,)),
            pltpu.SemaphoreType.DMA,
        ],
        compiler_params=pltpu.CompilerParams(collective_id=0, has_side_effects=True),
        name="gather_hot",
    )(own)
    return full.reshape(-1, own.shape[1])


def update_kernel(
    dims, part, old, grad, full,
    twin, packed, in_a, in_b, sum_a, sum_b, in_a2, in_b2, line, in_z, fresh,
    send_sem, recv_sem, local_sem,
):
    me = Place(dims)
    n_hi, n_y, n_z, n_lo, _ = dims
    n_x = n_hi * n_lo
    half = n_z // 2
    low, top = pl.ds(0, half), pl.ds(half, half)
    me.meet()
    sender = Sender(send_sem, recv_sem)
    f32, bf16 = jnp.float32, jnp.bfloat16

    sender.start(part.at[:, :, :, :, 1 - me.c], twin, me.partner()).wait_recv()

    def add_twin(i, carry):
        x_hi, y, z = i // (n_y * n_z), (i // n_z) % n_y, i % n_z
        for x_lo in range(n_lo):
            total = part[x_hi, y, z, x_lo, me.c] + twin[x_hi, y, z, x_lo]
            twin[x_hi, y, z, x_lo] = total
            packed[x_hi, y, z, x_lo] = total.astype(bf16)
        return carry

    lax.fori_loop(0, n_hi * n_y * n_z, add_twin, 0)

    stage = []
    for k in range(1, n_x):
        x, device = me.along_x(k)
        src = packed.at[x // n_lo, :, low, x % n_lo]
        stage.append(sender.start(src, in_a.at[k - 1], device))
    for k in range(1, n_y):
        y, device = me.along_y(k)
        stage.append(sender.start(packed.at[:, y, top], in_b.at[k - 1], device))
    for copy in stage:
        copy.wait_recv()

    def add_plane(z, carry):
        for y in range(n_y):
            total = twin[me.x_hi, y, z, me.x_lo]
            for k in range(n_x - 1):
                total = total + in_a[k, y, z].astype(f32)
            sum_a[y, z] = total
        for x_hi in range(n_hi):
            for x_lo in range(n_lo):
                total = twin[x_hi, me.y, half + z, x_lo]
                for k in range(n_y - 1):
                    total = total + in_b[k, x_hi, z, x_lo].astype(f32)
                sum_b[x_hi, x_lo, z] = total
        return carry

    lax.fori_loop(0, half, add_plane, 0)

    stage = []
    for k in range(1, n_y):
        y, device = me.along_y(k)
        stage.append(sender.start(sum_a.at[y], in_a2.at[k - 1], device))
    for k in range(1, n_x):
        x, device = me.along_x(k)
        stage.append(sender.start(sum_b.at[x // n_lo, x % n_lo], in_b2.at[k - 1], device))
    for copy in stage:
        copy.wait_recv()

    def add_line(z, carry):
        total = sum_a[me.y, z]
        for k in range(n_y - 1):
            total = total + in_a2[k, z]
        line[z] = total
        total = sum_b[me.x_hi, me.x_lo, z]
        for k in range(n_x - 1):
            total = total + in_b2[k, z]
        line[half + z] = total
        return carry

    lax.fori_loop(0, half, add_line, 0)

    stage = []
    for k in range(1, n_z):
        z, device = me.along_z(k)
        stage.append(sender.start(line.at[z], in_z.at[k - 1], device))
    for copy in stage:
        copy.wait_recv()
    total = line[me.z]
    for k in range(n_z - 1):
        total = total + in_z[k]
    grad[...] = total
    fresh[...] = (old[...] - 0.1 * total).astype(bf16)

    gather_rows(me, fresh, full, sender, local_sem)
    sender.finish()


def update_hot(part, old, dims):
    n_hi, n_y, n_z, n_lo, _ = dims
    n_x, half = n_hi * n_lo, n_z // 2
    tile = old.shape
    f32, bf16 = jnp.float32, jnp.bfloat16
    count = copies_of_gather(dims) + copies_of_scatter(dims)
    grad, full = pl.pallas_call(
        functools.partial(update_kernel, dims),
        out_shape=(
            jax.ShapeDtypeStruct(tile, f32),
            jax.ShapeDtypeStruct((*dims, *tile), bf16),
        ),
        in_specs=[pl.BlockSpec(memory_space=pltpu.VMEM)] * 2,
        out_specs=(pl.BlockSpec(memory_space=pltpu.VMEM),) * 2,
        scratch_shapes=[
            pltpu.VMEM((n_hi, n_y, n_z, n_lo, *tile), f32),
            pltpu.VMEM((n_hi, n_y, n_z, n_lo, *tile), bf16),
            pltpu.VMEM((n_x - 1, n_y, half, *tile), bf16),
            pltpu.VMEM((n_y - 1, n_hi, half, n_lo, *tile), bf16),
            pltpu.VMEM((n_y, half, *tile), f32),
            pltpu.VMEM((n_hi, n_lo, half, *tile), f32),
            pltpu.VMEM((n_y - 1, half, *tile), f32),
            pltpu.VMEM((n_x - 1, half, *tile), f32),
            pltpu.VMEM((n_z, *tile), f32),
            pltpu.VMEM((n_z - 1, *tile), f32),
            pltpu.VMEM(tile, bf16),
            pltpu.SemaphoreType.DMA((count,)),
            pltpu.SemaphoreType.DMA((count,)),
            pltpu.SemaphoreType.DMA,
        ],
        compiler_params=pltpu.CompilerParams(collective_id=1, has_side_effects=True),
        name="update_hot",
    )(part.reshape(*dims, *tile), old)
    return grad, full.reshape(-1, tile[1])


def body(dims, table, hot_slot, cold_row, cold_bag, hot_pick, dense, label):
    n = math.prod(dims)
    n_table, width = table.shape
    samples = dense.shape[0]
    own_hot = hot_slot.shape[0]
    cap = cold_row.shape[2]
    slots = cold_row.shape[1] * cap
    f32, bf16 = jnp.float32, jnp.bfloat16
    rounded = table.astype(bf16)

    arrived = exchange(cold_row[0]).reshape(slots)
    hot_old = table[hot_slot]
    hot_copy = gather_hot(hot_old.astype(bf16), dims)

    row_ids = jnp.arange(n_table, dtype=jnp.int32)
    at_row = (arrived[:, None] == row_ids[None, :]).astype(bf16)
    looked = jnp.dot(at_row, rounded, preferred_element_type=f32).astype(bf16)
    returned = exchange(looked.reshape(n, cap, width)).reshape(slots, width)

    bags = cold_bag[0].reshape(slots)
    sample_ids = jnp.arange(samples, dtype=jnp.int32)
    selector = (sample_ids[:, None] == bags[None, :]).astype(bf16)
    hot_ids = jnp.arange(n * own_hot, dtype=jnp.int32)
    counts = sum(
        (hot_pick[:, j][:, None] == hot_ids[None, :]).astype(f32)
        for j in range(hot_pick.shape[1])
    ).astype(bf16)
    counts = lax.optimization_barrier(counts)
    hot_pooled = jnp.dot(counts, hot_copy, preferred_element_type=f32)
    pooled = jnp.dot(selector, returned, preferred_element_type=f32) + hot_pooled
    score = jnp.sum(pooled * dense, axis=1) / width**0.5
    err = jax.nn.sigmoid(score) - label.astype(f32)
    grad = err[:, None] * dense
    high, low = split_bf16(grad)

    first = (((0,), (0,)), ((), ()))
    slot_grad = lax.dot_general(selector, high, first, preferred_element_type=f32).astype(bf16)
    delivered = exchange(slot_grad.reshape(n, cap, width)).reshape(slots, width)

    hot_local = lax.dot_general(counts, high, first, preferred_element_type=f32)
    hot_local = hot_local + lax.dot_general(counts, low, first, preferred_element_type=f32)
    own_grad, hot_new = update_hot(hot_local, hot_old, dims)

    table_grad = lax.dot_general(at_row, delivered, first, preferred_element_type=f32)
    at_hot = (row_ids[:, None] == hot_slot[None, :]).astype(f32)
    table_grad = table_grad + jnp.dot(
        at_hot, own_grad, precision=lax.Precision.HIGHEST, preferred_element_type=f32
    )
    new_table = table - 0.1 * table_grad
    return (pooled, new_table, hot_new.astype(f32))


def solution(mesh, dims=SHAPE):
    placed = (
        P(AXES, None),
        P(AXES),
        P(AXES, None, None),
        P(AXES, None, None),
        P(AXES, None),
        P(AXES, None),
        P(AXES),
    )
    return jax.shard_map(
        functools.partial(body, dims),
        mesh=mesh,
        in_specs=placed,
        out_specs=(P(AXES, None), P(AXES, None), P()),
        check_vma=False,
    )
```

time: 300 us -> 183 us (0.61)
  waiting for transfers between devices: 204 us -> 0.01 us
  Pallas kernels: 0 us -> 99.8 us
  starting transfers between devices: 50.8 us -> 11.5 us
  blocking collectives: 0 us -> 28.3 us
  matrix products: 31.1 us -> 24 us
  other arithmetic: 4.46 us -> 10.3 us
    all_to_all x6 -> x2, waiting for transfers between devices: 204 us -> 0.01 us  [exchange(): return lax.all_to_all(blocks, AXES, split_axis=0, concat_axis=0, tiled=True)]
    pallas_call x0 -> x2, Pallas kernels: none -> 99.8 us  [the longest x1 60 us: update_hot(): pl.pallas_call(functools.partial(update_kernel, dims), out_shape=(jax.Sha...]
    all_to_all x6 -> x2, starting transfers between devices: 50.8 us -> 11.5 us  [exchange(): return lax.all_to_all(blocks, AXES, split_axis=0, concat_axis=0, tiled=True)]
    all_to_all x0 -> x1, blocking collectives: none -> 28.3 us  [exchange(): return lax.all_to_all(blocks, AXES, split_axis=0, concat_axis=0, tiled=True)]
    convert_element_type x3, other arithmetic: 2.49 us -> 9.34 us  [the longest x1 4.81 us: body(): counts = sum(((hot_pick[:, j][:, None] == hot_ids[None, :]).astype(f32) f...]
    dot_general x1, matrix products: 4.6 us -> 0.81 us  [body(): hot_local = lax.dot_general(counts, high, first, preferred_element_type=f32)]
    dot_general x1, matrix products: 6.34 us -> 2.91 us  [body(): lax.dot_general(counts, low, first, preferred_element_type=f32)]
  transfers between devices with their start and end apart: 6 -> 2, of which waited for: 6 -> 0; matrix products, arithmetic and copies ran while one was open for 8% -> 12% of each run, Pallas kernels for 0% -> 55%
where the time goes in v2:
time: 183 us; the launch traced here: 182 us
  Pallas kernels  99.8 us (55%)
  blocking collectives  28.3 us (15%)
  matrix products  24 us (13%)
  starting transfers between devices  11.5 us (6%)
  other arithmetic  10.3 us (6%)
  local copies, waits for them, and re-layouts  7.45 us (4%)
    pallas_call x1, Pallas kernels, update_hot(): pl.pallas_call(functools.partial(update_kernel, dims), out_shape=(jax.Sha...  60 us
    pallas_call x1, Pallas kernels, gather_hot(): pl.pallas_call(functools.partial(gather_kernel, dims), out_shape=jax.Shap...  39.8 us
    all_to_all x1, blocking collectives, exchange(): return lax.all_to_all(blocks, AXES, split_axis=0, concat_axis=0, tiled=True)  28.3 us
    all_to_all x2, starting transfers between devices, exchange(): return lax.all_to_all(blocks, AXES, split_axis=0, concat_axis=0, tiled=True)  11.5 us
    dot_general x1, matrix products, body(): looked = jnp.dot(at_row, rounded, preferred_element_type=f32).astype(bf16)  5.49 us
    dot_general x1, matrix products, body(): lax.dot_general(at_row, delivered, first, preferred_element_type=f32)  4.94 us
    convert_element_type x1, other arithmetic, body(): counts = sum(((hot_pick[:, j][:, None] == hot_ids[None, :]).astype(f32) f...  4.81 us
    unnamed x28, local copies, waits for them, and re-layouts  3.94 us
  transfers between devices with their start and end apart: 2, of which 0 were waited for; matrix products, arithmetic and copies ran while one was open for 12% of the time, Pallas kernels for 55%

profile of v2, /device:TPU:1, one launch (start us, length us, event | category | flops | bytes accessed | tf_op | source)
XLA Modules:
  0.0 182.2 jit_solution(16165914173098070811)
XLA Ops:
  0.6 0.8 copy.17
  1.5 28.3 %all_to_all.19 = s32[256,1,8]{2,1,0:T(1,128)S(1)} all-to-all(s32[256,1,8]{2,1,0:T(1,128)S(1)} %bitcast.33), channel_id=1, replica_groups=mesh['rows'=64,'grp'=4] {'rows','grp'}, dimensions={0} | all-to-all | bytes 16384 | tf_op jit(solution)/shard_map/all_to_all | solution.py:17
  29.7 0.5 broadcast.25
  30.2 1.0 reduce.3
  31.2 0.1 eq.167
  31.3 0.0 copy-start.6
  31.3 0.6 copy-done.6
  31.9 0.0 copy-start.8
  31.9 5.5 %fusion.9 = bf16[256,8,256]{2,1,0:T(8,128)(2,1)} fusion(s32[2048]{0:T(1024)S(1)} %eq.167, f32[2048,256]{1,0:T(8,128)} %param.7), kind=kOutput, calls=%fused_computation.25 | convolution fusion | flops 2152726528 | bytes 3153920 | tf_op jit(solution)/shard_map/dot_general | solution.py:297
  37.4 0.0 copy-start.10
  37.4 0.0 copy-start
  37.4 6.2 %all-to-all-start.1 = ((bf16[256,8,256]{2,1,0:T(8,128)(2,1)}), bf16[256,8,256]{2,1,0:T(8,128)(2,1)S(1)}, u32[]{:S(2)}, u32[]{:S(2)}) async-start(bf16[256,8,256]{2,1,0:T(8,128)(2,1)} %fusion.9), calls=%async_computation.1 | async-start | bytes 2097152 | tf_op jit(solution)/shard_map/all_to_all | solution.py:17
  43.6 0.0 copy-done.8
  43.6 4.8 %add_convert_fusion = bf16[256,4096]{1,0:T(8,128)(2,1)S(1)} fusion(s32[256]{0:T(256)S(1)} %bitcast.40, s32[256]{0:T(256)S(1)} %bitcast.41, s32[256]{0:T(256)S(1)} %bitcast.35, s32[256]{0:T(256)S(1)} %bitcast.36, s32[256]{0:T(256)S(1)} %bitcast.37, s32[256]{0:T(256)S(1)} %bitcast.38, s32[256]{0:T(256)S(1)} %bitcast.39, s32[256]{0:T(256)S(1)} %bitcast.34), kind=kLoop, calls=%fused_computation.7 | loop fusion | flops 25165824 | bytes 2105344 | tf_op jit(solution)/shard_map/convert_element_type | solution.py:307
  48.4 0.0 copy-done.10
  48.5 2.2 %gather_fusion = f32[16,256]{1,0:T(8,128)S(1)} fusion(f32[2048,256]{1,0:T(8,128)} %param.7, s32[1024]{0:T(1024)S(1)} %pad_clamp_fusion), kind=kCustom, calls=%fused_computation | custom fusion | bytes 32832 | tf_op jit(solution)/shard_map/gather | solution.py:292
  50.6 0.0 copy-start.3
  50.6 0.6 convert_element_type.68.own
  51.2 39.8 %gather_hot.1 = bf16[2,4,8,2,2,16,256]{6,5,4,3,2,1,0:T(8,128)(2,1)} custom-call(bf16[16,256]{1,0:T(8,128)(2,1)} %convert_element_type.68.own), custom_call_target="tpu_custom_call" | custom-call | tf_op jit(solution)/shard_map/gather_hot/pallas_call | solution.py:137
  91.0 0.8 copy.16
  91.9 0.7 eq.164
  92.6 0.0 copy-done
  92.6 0.0 copy-start.4
  92.6 0.0 copy-start.9
  92.6 0.8 copy.18
  93.4 3.2 %fusion.22 = f32[256,256]{0,1:T(8,128)} fusion(bf16[256,4096]{1,0:T(8,128)(2,1)S(1)} %add_convert_fusion, bf16[4096,256]{1,0:T(8,128)(2,1)} %bitcast.32), kind=kOutput, calls=%fused_computation.44 | convolution fusion | flops 536870912 | bytes 4456448 | tf_op jit(solution)/shard_map/dot_general | solution.py:309
  96.6 0.0 all-to-all-done.1
  96.6 0.0 copy-done.4
  96.6 2.4 %multiply_reduce_fusion = (f32[256]{0:T(256)S(1)}, f32[256,256]{0,1:T(8,128)}) fusion(f32[256,256]{0,1:T(8,128)} %copy.18, f32[256,256]{0,1:T(8,128)} %fusion.22, bf16[256,8,256]{2,1,0:T(8,128)(2,1)S(1)} %all-to-all-done.1, s32[2048]{0:T(1024)S(1)} %copy-done.4), kind=kOutput, calls=%fused_computation.37 | convolution fusion | flops 269156096 | bytes 1844224 | tf_op jit(solution)/shard_map/dot_general | solution.py:310
  99.1 0.0 copy-done.3
  99.1 0.0 copy-done.9
  99.1 1.8 fusion.8
  100.9 5.4 %all-to-all-start.2 = ((bf16[256,8,256]{2,1,0:T(8,128)(2,1)}), bf16[256,8,256]{2,1,0:T(8,128)(2,1)S(1)}, u32[]{:S(2)}, u32[]{:S(2)}) async-start(bf16[256,8,256]{2,1,0:T(8,128)(2,1)} %fusion.8), calls=%async_computation.2 | async-start | bytes 2097152 | tf_op jit(solution)/shard_map/all_to_all | solution.py:17
  106.2 0.8 fusion.20
  107.1 2.9 %convolution_add_fusion = f32[4096,256]{1,0:T(8,128)} fusion(f32[4096,256]{1,0:T(8,128)S(1)} %fusion.20, bf16[256,4096]{1,0:T(8,128)(2,1)S(1)} %add_convert_fusion, f32[256,256]{1,0:T(8,128)S(1)} %copy-done, f32[256]{0:T(256)S(1)} %divide_subtract_fusion), kind=kOutput, calls=%fused_computation.6 | convolution fusion | flops 538181632 | bytes 10748928 | tf_op jit(solution)/shard_map/dot_general | solution.py:321
  110.0 0.0 copy-start.2
  110.0 60.0 %update_hot.1 = (f32[16,256]{1,0:T(8,128)}, bf16[2,4,8,2,2,16,256]{6,5,4,3,2,1,0:T(8,128)(2,1)}) custom-call(f32[2,4,8,2,2,16,256]{6,5,4,3,2,1,0:T(8,128)} %bitcast.31, f32[16,256]{1,0:T(8,128)} %copy-done.3), custom_call_target="tpu_custom_call" | custom-call | tf_op jit(solution)/shard_map/update_hot/pallas_call | solution.py:251
  170.0 0.0 copy-start.7
  170.0 0.0 copy-done.2
  170.0 0.8 copy.19
  170.9 3.9 %bitcast_convert_fusion = f32[4096,256]{1,0:T(8,128)} fusion(bf16[2,4,8,2,2,16,256]{6,5,4,3,2,1,0:T(8,128)(2,1)} %get-tuple-element.6), kind=kLoop, calls=%fused_computation.21 | loop fusion | flops 1048576 | bytes 6291456 | tf_op jit(solution)/shard_map/convert_element_type | solution.py:330
  174.8 0.0 all-to-all-done.2
  174.8 0.0 copy-done.7
  174.8 4.9 %fusion = f32[2048,256]{1,0:T(8,128)S(1)} fusion(s32[2048]{0:T(1024)S(1)} %copy-done.7, bf16[256,8,256]{2,1,0:T(8,128)(2,1)S(1)} %all-to-all-done.2), kind=kOutput, calls=%fused_computation.2 | convolution fusion | flops 2151677952 | bytes 3153920 | tf_op jit(solution)/shard_map/dot_general | solution.py:324
  179.8 0.0 copy-done.1
  179.8 0.0 copy-done.5
  179.8 0.0 copy-done.11
  179.8 2.4 %fusion.5 = f32[2048,256]{1,0:T(8,128)} fusion(f32[2048,256]{1,0:T(8,128)S(1)} %copy-done.1, f32[2048,256]{1,0:T(8,128)S(1)} %fusion, f32[16,256]{1,0:T(8,128)S(1)} %copy-done.5, s32[16]{0:T(128)S(1)} %copy-done.11), kind=kOutput, calls=%fused_computation.18 | convolution fusion | flops 102268928 | bytes 6307904 | tf_op jit(solution)/shard_map/dot_general | solution.py:326
  (7 shorter events, 0.0 us)
Async XLA Ops:
  31.3 0.6 copy-start.6
  31.9 11.7 %copy-start.8 = (s32[256,8]{0,1:T(8,128)S(1)}, s32[256,8]{0,1:T(8,128)}, u32[]{:S(2)}) copy-start(s32[256,8]{0,1:T(8,128)} %param.11) | copy-start | bytes 24580
  37.4 11.0 %copy-start.10 = (s32[16]{0:T(128)S(1)}, s32[16]{0:T(128)}, u32[]{:S(2)}) copy-start(s32[16]{0:T(128)} %param.8) | copy-start | bytes 196
  37.4 55.2 %copy-start = (f32[256,256]{1,0:T(8,128)S(1)}, f32[256,256]{1,0:T(8,128)}, u32[]{:S(2)}) copy-start(f32[256,256]{1,0:T(8,128)} %param.12) | copy-start | bytes 786436
  37.4 59.2 %all-to-all-start.1 = ((bf16[256,8,256]{2,1,0:T(8,128)(2,1)}), bf16[256,8,256]{2,1,0:T(8,128)(2,1)S(1)}, u32[]{:S(2)}, u32[]{:S(2)}) async-start(bf16[256,8,256]{2,1,0:T(8,128)(2,1)} %fusion.9), calls=%async_computation.1 | async-start | bytes 2097152 | tf_op jit(solution)/shard_map/all_to_all | solution.py:17
  50.6 48.5 %copy-start.3 = (f32[16,256]{1,0:T(8,128)}, f32[16,256]{1,0:T(8,128)S(1)}, u32[]{:S(2)}) copy-start(f32[16,256]{1,0:T(8,128)S(1)} %gather_fusion) | copy-start | bytes 49156
  92.6 4.1 %copy-start.4 = (s32[2048]{0:T(1024)S(1)}, s32[2048]{0:T(1024)}, u32[]{:S(2)}) copy-start(s32[2048]{0:T(1024)} %eq.164) | copy-start | bytes 24580
  92.6 6.5 %copy-start.9 = (s32[256]{0:T(256)S(1)}, s32[256]{0:T(256)}, u32[]{:S(2)}) copy-start(s32[256]{0:T(256)} %param.13) | copy-start | bytes 3076
  100.9 73.9 %all-to-all-start.2 = ((bf16[256,8,256]{2,1,0:T(8,128)(2,1)}), bf16[256,8,256]{2,1,0:T(8,128)(2,1)S(1)}, u32[]{:S(2)}, u32[]{:S(2)}) async-start(bf16[256,8,256]{2,1,0:T(8,128)(2,1)} %fusion.8), calls=%async_computation.2 | async-start | bytes 2097152 | tf_op jit(solution)/shard_map/all_to_all | solution.py:17
  110.0 60.1 %copy-start.2 = (f32[256,256]{0,1:T(8,128)S(1)}, f32[256,256]{0,1:T(8,128)}, u32[]{:S(2)}) copy-start(f32[256,256]{0,1:T(8,128)} %get-tuple-element.25) | copy-start | bytes 786436
  170.0 4.8 %copy-start.7 = (s32[2048]{0:T(1024)S(1)}, s32[2048]{0:T(1024)}, u32[]{:S(2)}) copy-start(s32[2048]{0:T(1024)} %copy-done.6) | copy-start | bytes 24580
  174.8 5.0 %copy-start.1 = (f32[2048,256]{1,0:T(8,128)S(1)}, f32[2048,256]{1,0:T(8,128)}, u32[]{:S(2)}) copy-start(f32[2048,256]{1,0:T(8,128)} %param.7) | copy-start | bytes 6291460
  174.8 5.0 %copy-start.5 = (f32[16,256]{1,0:T(8,128)S(1)}, f32[16,256]{1,0:T(8,128)}, u32[]{:S(2)}) copy-start(f32[16,256]{1,0:T(8,128)} %get-tuple-element.5) | copy-start | bytes 49156
  174.8 5.0 %copy-start.11 = (s32[16]{0:T(128)S(1)}, s32[16]{0:T(128)}, u32[]{:S(2)}) copy-start(s32[16]{0:T(128)} %param.8) | copy-start | bytes 196

commit v3 on v2

--- a/solution.py
+++ b/solution.py
@@ -61,15 +61,6 @@
         for peer in peers:
             pl.semaphore_signal(barrier, inc=1, device_id=peer, device_id_type=MESH)
         pl.semaphore_wait(barrier, len(peers))
-
-
-def copies_of_gather(dims):
-    n_x, n_y, n_z = dims[0] * dims[3], dims[1], dims[2]
-    return (n_z - 1) + 2 * (n_y - 1) + 2 * (n_x - 1) + 1
-
-
-def copies_of_scatter(dims):
-    return copies_of_gather(dims)
 
 
 class Sender:
@@ -97,63 +88,180 @@
             copy.wait_send()
 
 
-def gather_rows(me, own, full, sender, local_sem):
+def spread_lines(me, own, line, plane_a, plane_b, sender, near):
     n_x, n_y, n_z = me.n
     half = n_z // 2
-    mine = full.at[me.x_hi, me.y, me.z, me.x_lo, me.c]
-    keep = pltpu.make_async_copy(own, mine, local_sem)
-    keep.start()
-    stage = [sender.start(own, mine, me.along_z(k)[1]) for k in range(1, n_z)]
+    low, top = pl.ds(0, half), pl.ds(half, half)
+    keep = near.start(own, line.at[me.z])
+    stage = [sender.start(own, line.at[me.z], me.along_z(k)[1]) for k in range(1, n_z)]
+    yield
     keep.wait()
     for copy in stage:
         copy.wait_recv()
+    to_a, to_b = plane_a.at[me.y], plane_b.at[me.x_hi, :, me.x_lo]
+    stage = [sender.start(line.at[low], to_a, me.along_y(k)[1]) for k in range(1, n_y)]
+    stage += [sender.start(line.at[top], to_b, me.along_x(k)[1]) for k in range(1, n_x)]
+    keep = [near.start(line.at[low], to_a), near.start(line.at[top], to_b)]
+    yield
+    for copy in keep:
+        copy.wait()
+    for copy in stage:
+        copy.wait_recv()
+    yield
+
+
+def spread_planes(me, plane_a, plane_b, full, sender, near):
+    n_x, n_y, n_z = me.n
+    n_lo = me.dims[3]
+    half = n_z // 2
     low, top = pl.ds(0, half), pl.ds(half, half)
-    line = full.at[me.x_hi, me.y, low, me.x_lo, me.c]
-    stage = [sender.start(line, line, me.along_y(k)[1]) for k in range(1, n_y)]
-    line = full.at[me.x_hi, me.y, top, me.x_lo, me.c]
-    stage += [sender.start(line, line, me.along_x(k)[1]) for k in range(1, n_x)]
-    for copy in stage:
-        copy.wait_recv()
-    plane = full.at[me.x_hi, :, low, me.x_lo, me.c]
-    stage = [sender.start(plane, plane, me.along_x(k)[1]) for k in range(1, n_x)]
-    plane = full.at[:, me.y, top, :, me.c]
-    stage += [sender.start(plane, plane, me.along_y(k)[1]) for k in range(1, n_y)]
-    for copy in stage:
-        copy.wait_recv()
-    side = full.at[:, :, :, :, me.c]
-    sender.start(side, side, me.partner()).wait_recv()
-
-
-def gather_kernel(dims, own, full, send_sem, recv_sem, local_sem):
+
+    def of_x(x):
+        return full.at[x // n_lo, :, low, x % n_lo, me.c]
+
+    def of_y(y):
+        return full.at[:, y, top, :, me.c]
+
+    over_x = [sender.start(plane_a, of_x(me.x), me.along_x(k)[1]) for k in range(1, n_x)]
+    over_y = [sender.start(plane_b, of_y(me.y), me.along_y(k)[1]) for k in range(1, n_y)]
+    side = [
+        sender.start(plane_a, of_x(me.x), me.partner()),
+        sender.start(plane_b, of_y(me.y), me.partner()),
+    ]
+    keep = [near.start(plane_a, of_x(me.x)), near.start(plane_b, of_y(me.y))]
+    arrivals = [(copy, of_x((me.x + n_x - k) % n_x)) for k, copy in enumerate(over_x, 1)]
+    arrivals += [(copy, of_y((me.y + n_y - k) % n_y)) for k, copy in enumerate(over_y, 1)]
+    for copy, landed in arrivals:
+        copy.wait_recv()
+        side.append(sender.start(landed, landed, me.partner()))
+    for copy in keep:
+        copy.wait()
+    for copy in side:
+        copy.wait_recv()
+
+
+class Near:
+    def __init__(self, sem):
+        self.sem, self.used = sem, 0
+
+    def start(self, src, dst):
+        copy = pltpu.make_async_copy(src, dst, self.sem.at[self.used])
+        copy.start()
+        self.used += 1
+        return copy
+
+
+SEMS = [pltpu.SemaphoreType.DMA((64,)), pltpu.SemaphoreType.DMA((64,)), pltpu.SemaphoreType.DMA((8,))]
+IN_VMEM = pl.BlockSpec(memory_space=pltpu.VMEM)
+
+
+def request_kernel(
+    dims, width, asks, own, got, plane_a, plane_b, from_z, from_y, line,
+    send_sem, recv_sem, near_sem,
+):
+    me = Place(dims)
+    n_x, n_y, n_z = me.n
+    me.meet()
+    sender, near = Sender(send_sem, recv_sem), Near(near_sem)
+
+    keep = near.start(asks.at[me.z], from_z.at[me.z])
+    stage = []
+    for k in range(1, n_z):
+        z, device = me.along_z(k)
+        stage.append(sender.start(asks.at[z], from_z.at[me.z], device))
+    lines = spread_lines(me, own, line, plane_a, plane_b, sender, near)
+    next(lines)
+    keep.wait()
+    for copy in stage:
+        copy.wait_recv()
+
+    def of_y(y):
+        return from_z.at[:, y * width // 128]
+
+    keep = near.start(of_y(me.y), from_y.at[me.y])
+    stage = []
+    for k in range(1, n_y):
+        y, device = me.along_y(k)
+        stage.append(sender.start(of_y(y), from_y.at[me.y], device))
+    next(lines)
+    keep.wait()
+    for copy in stage:
+        copy.wait_recv()
+
+    mine = got.at[me.c, me.x]
+    keep = near.start(from_y, mine)
+    stage = [sender.start(from_y, mine, me.along_x(k)[1]) for k in range(1, n_x)]
+    keep.wait()
+    for copy in stage:
+        copy.wait_recv()
+    side = sender.start(got.at[me.c], got.at[me.c], me.partner())
+    next(lines)
+    side.wait_recv()
+    sender.finish()
+
+
+def request_rows(rows, own, dims):
+    n_hi, n_y, n_z, n_lo, n_core = dims
+    n_x, half = n_hi * n_lo, n_z // 2
+    cap = rows.shape[1]
+    width = n_x * n_core * cap
+    tiles = -(-n_y * width // 128)
+    asks = rows.reshape(*dims, cap).transpose(2, 1, 0, 3, 4, 5).reshape(n_z, n_y * width)
+    asks = jnp.pad(asks, ((0, 0), (0, tiles * 128 - n_y * width)))
+    got, plane_a, plane_b = pl.pallas_call(
+        functools.partial(request_kernel, dims, width),
+        out_shape=(
+            jax.ShapeDtypeStruct((n_core, n_x, n_y, n_z, 1, 128), jnp.int32),
+            jax.ShapeDtypeStruct((n_y, half, *own.shape), own.dtype),
+            jax.ShapeDtypeStruct((n_hi, half, n_lo, *own.shape), own.dtype),
+        ),
+        in_specs=[IN_VMEM] * 2,
+        out_specs=(IN_VMEM,) * 3,
+        scratch_shapes=[
+            pltpu.VMEM((n_z, tiles, 1, 128), jnp.int32),
+            pltpu.VMEM((n_y, n_z, 1, 128), jnp.int32),
+            pltpu.VMEM((n_z, *own.shape), own.dtype),
+            *SEMS,
+        ],
+        compiler_params=pltpu.CompilerParams(collective_id=0, has_side_effects=True),
+        name="request_rows",
+    )(asks.reshape(n_z, tiles, 1, 128), own)
+    r, g = lax.axis_index("rows"), lax.axis_index("grp")
+    y = lax.rem(lax.div(r, n_z), n_y)
+    pair = lax.div(r, n_y * n_z) * (n_lo * n_core) + g
+    lane = lax.rem(y * width, 128) + pair * cap
+    got = lax.dynamic_slice_in_dim(got.reshape(-1, 128), lane, cap, axis=1)
+    got = got.reshape(n_core, n_hi, n_lo, n_y, n_z, cap).transpose(1, 3, 4, 2, 0, 5)
+    return got.reshape(-1), plane_a, plane_b
+
+
+def finish_kernel(dims, plane_a, plane_b, full, send_sem, recv_sem, near_sem):
     me = Place(dims)
     me.meet()
-    sender = Sender(send_sem, recv_sem)
-    gather_rows(me, own, full, sender, local_sem)
+    sender, near = Sender(send_sem, recv_sem), Near(near_sem)
+    spread_planes(me, plane_a, plane_b, full, sender, near)
     sender.finish()
 
 
-def gather_hot(own, dims):
-    count = copies_of_gather(dims)
+def finish_gather(plane_a, plane_b, dims):
+    tile = plane_a.shape[-2:]
     full = pl.pallas_call(
-        functools.partial(gather_kernel, dims),
-        out_shape=jax.ShapeDtypeStruct((*dims, *own.shape), own.dtype),
-        in_specs=[pl.BlockSpec(memory_space=pltpu.VMEM)],
-        out_specs=pl.BlockSpec(memory_space=pltpu.VMEM),
-        scratch_shapes=[
-            pltpu.SemaphoreType.DMA((count,)),
-            pltpu.SemaphoreType.DMA((count,)),
-            pltpu.SemaphoreType.DMA,
-        ],
-        compiler_params=pltpu.CompilerParams(collective_id=0, has_side_effects=True),
-        name="gather_hot",
-    )(own)
-    return full.reshape(-1, own.shape[1])
+        functools.partial(finish_kernel, dims),
+        out_shape=jax.ShapeDtypeStruct((*dims, *tile), plane_a.dtype),
+        in_specs=[IN_VMEM] * 2,
+        out_specs=IN_VMEM,
+        scratch_shapes=SEMS,
+        compiler_params=pltpu.CompilerParams(collective_id=2, has_side_effects=True),
+        name="finish_gather",
+    )(plane_a, plane_b)
+    return full.reshape(-1, tile[1])
 
 
 def update_kernel(
     dims, part, old, grad, full,
-    twin, packed, in_a, in_b, sum_a, sum_b, in_a2, in_b2, line, in_z, fresh,
-    send_sem, recv_sem, local_sem,
+    twin_a, twin_b, packed_a, packed_b, in_a, in_b, in_a2, in_b2,
+    line, in_z, fresh, spread, plane_a, plane_b,
+    send_sem, recv_sem, near_sem,
 ):
     me = Place(dims)
     n_hi, n_y, n_z, n_lo, _ = dims
@@ -161,44 +269,65 @@
     half = n_z // 2
     low, top = pl.ds(0, half), pl.ds(half, half)
     me.meet()
-    sender = Sender(send_sem, recv_sem)
+    sender, near = Sender(send_sem, recv_sem), Near(near_sem)
     f32, bf16 = jnp.float32, jnp.bfloat16
 
-    sender.start(part.at[:, :, :, :, 1 - me.c], twin, me.partner()).wait_recv()
-
-    def add_twin(i, carry):
-        x_hi, y, z = i // (n_y * n_z), (i // n_z) % n_y, i % n_z
-        for x_lo in range(n_lo):
-            total = part[x_hi, y, z, x_lo, me.c] + twin[x_hi, y, z, x_lo]
-            twin[x_hi, y, z, x_lo] = total
-            packed[x_hi, y, z, x_lo] = total.astype(bf16)
-        return carry
-
-    lax.fori_loop(0, n_hi * n_y * n_z, add_twin, 0)
+    chunks = []
+    for k in [*range(1, max(n_x, n_y)), 0]:
+        if k < n_x:
+            x = me.along_x(k)[0]
+            src = part.at[x // n_lo, :, low, x % n_lo, 1 - me.c]
+            chunks.append((True, k, sender.start(src, twin_a.at[k], me.partner())))
+        if k < n_y:
+            y = me.along_y(k)[0]
+            src = part.at[:, y, top, :, 1 - me.c]
+            chunks.append((False, k, sender.start(src, twin_b.at[k], me.partner())))
 
     stage = []
-    for k in range(1, n_x):
-        x, device = me.along_x(k)
-        src = packed.at[x // n_lo, :, low, x % n_lo]
-        stage.append(sender.start(src, in_a.at[k - 1], device))
-    for k in range(1, n_y):
-        y, device = me.along_y(k)
-        stage.append(sender.start(packed.at[:, y, top], in_b.at[k - 1], device))
+    for is_a, k, copy in chunks:
+        copy.wait_recv()
+        x, to_x = me.along_x(k)
+        y, to_y = me.along_y(k)
+
+        def add_a(z, carry):
+            for j in range(n_y):
+                total = part[x // n_lo, j, z, x % n_lo, me.c] + twin_a[k, j, z]
+                if k:
+                    packed_a[k - 1, j, z] = total.astype(bf16)
+                else:
+                    twin_a[k, j, z] = total
+            return carry
+
+        def add_b(z, carry):
+            for i in range(n_hi):
+                for j in range(n_lo):
+                    total = part[i, y, half + z, j, me.c] + twin_b[k, i, z, j]
+                    if k:
+                        packed_b[k - 1, i, j, z] = total.astype(bf16)
+                    else:
+                        twin_b[k, i, z, j] = total
+            return carry
+
+        lax.fori_loop(0, half, add_a if is_a else add_b, 0)
+        if k and is_a:
+            stage.append(sender.start(packed_a.at[k - 1], in_a.at[k - 1], to_x))
+        elif k:
+            stage.append(sender.start(packed_b.at[k - 1], in_b.at[k - 1], to_y))
     for copy in stage:
         copy.wait_recv()
 
     def add_plane(z, carry):
-        for y in range(n_y):
-            total = twin[me.x_hi, y, z, me.x_lo]
+        for j in range(n_y):
+            total = twin_a[0, j, z]
             for k in range(n_x - 1):
-                total = total + in_a[k, y, z].astype(f32)
-            sum_a[y, z] = total
-        for x_hi in range(n_hi):
-            for x_lo in range(n_lo):
-                total = twin[x_hi, me.y, half + z, x_lo]
+                total = total + in_a[k, j, z].astype(f32)
+            twin_a[0, j, z] = total
+        for i in range(n_hi):
+            for j in range(n_lo):
+                total = twin_b[0, i, z, j]
                 for k in range(n_y - 1):
-                    total = total + in_b[k, x_hi, z, x_lo].astype(f32)
-                sum_b[x_hi, x_lo, z] = total
+                    total = total + in_b[k, i, j, z].astype(f32)
+                twin_b[0, i, z, j] = total
         return carry
 
     lax.fori_loop(0, half, add_plane, 0)
@@ -206,19 +335,20 @@
     stage = []
     for k in range(1, n_y):
         y, device = me.along_y(k)
-        stage.append(sender.start(sum_a.at[y], in_a2.at[k - 1], device))
+        stage.append(sender.start(twin_a.at[0, y], in_a2.at[k - 1], device))
     for k in range(1, n_x):
         x, device = me.along_x(k)
-        stage.append(sender.start(sum_b.at[x // n_lo, x % n_lo], in_b2.at[k - 1], device))
+        src = twin_b.at[0, x // n_lo, :, x % n_lo]
+        stage.append(sender.start(src, in_b2.at[k - 1], device))
     for copy in stage:
         copy.wait_recv()
 
     def add_line(z, carry):
-        total = sum_a[me.y, z]
+        total = twin_a[0, me.y, z]
         for k in range(n_y - 1):
             total = total + in_a2[k, z]
         line[z] = total
-        total = sum_b[me.x_hi, me.x_lo, z]
+        total = twin_b[0, me.x_hi, z, me.x_lo]
         for k in range(n_x - 1):
             total = total + in_b2[k, z]
         line[half + z] = total
@@ -238,7 +368,9 @@
     grad[...] = total
     fresh[...] = (old[...] - 0.1 * total).astype(bf16)
 
-    gather_rows(me, fresh, full, sender, local_sem)
+    for _ in spread_lines(me, fresh, spread, plane_a, plane_b, sender, near):
+        pass
+    spread_planes(me, plane_a, plane_b, full, sender, near)
     sender.finish()
 
 
@@ -247,30 +379,30 @@
     n_x, half = n_hi * n_lo, n_z // 2
     tile = old.shape
     f32, bf16 = jnp.float32, jnp.bfloat16
-    count = copies_of_gather(dims) + copies_of_scatter(dims)
     grad, full = pl.pallas_call(
         functools.partial(update_kernel, dims),
         out_shape=(
             jax.ShapeDtypeStruct(tile, f32),
             jax.ShapeDtypeStruct((*dims, *tile), bf16),
         ),
-        in_specs=[pl.BlockSpec(memory_space=pltpu.VMEM)] * 2,
-        out_specs=(pl.BlockSpec(memory_space=pltpu.VMEM),) * 2,
+        in_specs=[IN_VMEM] * 2,
+        out_specs=(IN_VMEM,) * 2,
         scratch_shapes=[
-            pltpu.VMEM((n_hi, n_y, n_z, n_lo, *tile), f32),
-            pltpu.VMEM((n_hi, n_y, n_z, n_lo, *tile), bf16),
+            pltpu.VMEM((n_x, n_y, half, *tile), f32),
+            pltpu.VMEM((n_y, n_hi, half, n_lo, *tile), f32),
             pltpu.VMEM((n_x - 1, n_y, half, *tile), bf16),
-            pltpu.VMEM((n_y - 1, n_hi, half, n_lo, *tile), bf16),
-            pltpu.VMEM((n_y, half, *tile), f32),
-            pltpu.VMEM((n_hi, n_lo, half, *tile), f32),
+            pltpu.VMEM((n_y - 1, n_hi, n_lo, half, *tile), bf16),
+            pltpu.VMEM((n_x - 1, n_y, half, *tile), bf16),
+            pltpu.VMEM((n_y - 1, n_hi, n_lo, half, *tile), bf16),
             pltpu.VMEM((n_y - 1, half, *tile), f32),
             pltpu.VMEM((n_x - 1, half, *tile), f32),
             pltpu.VMEM((n_z, *tile), f32),
             pltpu.VMEM((n_z - 1, *tile), f32),
             pltpu.VMEM(tile, bf16),
-            pltpu.SemaphoreType.DMA((count,)),
-            pltpu.SemaphoreType.DMA((count,)),
-            pltpu.SemaphoreType.DMA,
+            pltpu.VMEM((n_z, *tile), bf16),
+            pltpu.VMEM((n_y, half, *tile), bf16),
+            pltpu.VMEM((n_hi, half, n_lo, *tile), bf16),
+            *SEMS,
         ],
         compiler_params=pltpu.CompilerParams(collective_id=1, has_side_effects=True),
         name="update_hot",
@@ -288,9 +420,8 @@
     f32, bf16 = jnp.float32, jnp.bfloat16
     rounded = table.astype(bf16)
 
-    arrived = exchange(cold_row[0]).reshape(slots)
     hot_old = table[hot_slot]
-    hot_copy = gather_hot(hot_old.astype(bf16), dims)
+    arrived, plane_a, plane_b = request_rows(cold_row[0], hot_old.astype(bf16), dims)
 
     row_ids = jnp.arange(n_table, dtype=jnp.int32)
     at_row = (arrived[:, None] == row_ids[None, :]).astype(bf16)
@@ -306,6 +437,7 @@
         for j in range(hot_pick.shape[1])
     ).astype(bf16)
     counts = lax.optimization_barrier(counts)
+    hot_copy = finish_gather(plane_a, plane_b, dims)
     hot_pooled = jnp.dot(counts, hot_copy, preferred_element_type=f32)
     pooled = jnp.dot(selector, returned, preferred_element_type=f32) + hot_pooled
     score = jnp.sum(pooled * dense, axis=1) / width**0.5

time: 183 us -> 166 us (0.907)
  blocking collectives: 28.3 us -> 0 us
  Pallas kernels: 99.8 us -> 109 us
  starting transfers between devices: 11.5 us -> 15.2 us
    all_to_all x1 -> x0, blocking collectives: 28.3 us -> none  [exchange(): return lax.all_to_all(blocks, AXES, split_axis=0, concat_axis=0, tiled=True)]
    pallas_call x1 -> x2, Pallas kernels: 39.8 us -> 51 us  [the longest x1 25.6 us: finish_gather(): pl.pallas_call(functools.partial(finish_kernel, dims), out_shape=jax.Shap...]
    all_to_all x2, starting transfers between devices: 11.5 us -> 15.2 us  [exchange(): return lax.all_to_all(blocks, AXES, split_axis=0, concat_axis=0, tiled=True)]
    pallas_call x1, Pallas kernels: 60 us -> 57.6 us  [update_hot(): pl.pallas_call(functools.partial(update_kernel, dims), out_shape=(jax.Sha...]
    unnamed x28 -> x22, local copies, waits for them, and re-layouts: 3.94 us -> 2.65 us
  transfers between devices with their start and end apart: 2 -> 2, of which waited for: 0 -> 0; matrix products, arithmetic and copies ran while one was open for 12% -> 11% of each run, Pallas kernels for 55% -> 50%
where the time goes in v3:
time: 166 us
  Pallas kernels  109 us (66%)
  matrix products  24 us (14%)
  starting transfers between devices  15.2 us (9%)
  other arithmetic  10 us (6%)
  local copies, waits for them, and re-layouts  7.31 us (4%)
    pallas_call x1, Pallas kernels, update_hot(): pl.pallas_call(functools.partial(update_kernel, dims), out_shape=(jax.Sha...  57.6 us
    pallas_call x1, Pallas kernels, finish_gather(): pl.pallas_call(functools.partial(finish_kernel, dims), out_shape=jax.Shap...  25.6 us
    pallas_call x1, Pallas kernels, request_rows(): pl.pallas_call(functools.partial(request_kernel, dims, width), out_shape=...  25.4 us
    all_to_all x2, starting transfers between devices, exchange(): return lax.all_to_all(blocks, AXES, split_axis=0, concat_axis=0, tiled=True)  15.2 us
    dot_general x1, matrix products, body(): looked = jnp.dot(at_row, rounded, preferred_element_type=f32).astype(bf16)  5.5 us
    dot_general x1, matrix products, body(): lax.dot_general(at_row, delivered, first, preferred_element_type=f32)  4.94 us
    convert_element_type x1, other arithmetic, body(): counts = sum(((hot_pick[:, j][:, None] == hot_ids[None, :]).astype(f32) f...  4.81 us
    convert_element_type x1, other arithmetic, body(): return (pooled, new_table, hot_new.astype(f32))  3.93 us
  transfers between devices with their start and end apart: 2, of which 0 were waited for; matrix products, arithmetic and copies ran while one was open for 11% of the time, Pallas kernels for 50%

profile of v3, /device:TPU:1, one launch (start us, length us, event | category | flops | bytes accessed | tf_op | source)
XLA Modules:
  0.0 165.9 jit_solution(1608532856438768543)
XLA Ops:
  0.7 0.7 compare_select_fusion
  1.3 2.2 %gather_fusion = f32[16,256]{1,0:T(8,128)S(1)} fusion(f32[2048,256]{1,0:T(8,128)} %param.7, s32[1024]{0:T(1024)S(1)} %pad_clamp_fusion), kind=kCustom, calls=%fused_computation | custom fusion | bytes 32832 | tf_op jit(solution)/shard_map/gather | solution.py:423
  3.5 0.0 copy-start.3
  3.5 0.6 convert_element_type.57.own
  4.1 0.8 copy.19
  5.0 0.8 reshape.42.asks
  5.8 25.4 %request_rows.1 = (s32[2,4,4,8,1,128]{5,4,3,2,1,0:T(1,128)}, bf16[4,4,16,256]{3,2,1,0:T(8,128)(2,1)}, bf16[2,4,2,16,256]{4,3,2,1,0:T(8,128)(2,1)}) custom-call(s32[8,2,1,128]{3,2,1,0:T(1,128)} %reshape.42.asks, bf16[16,256]{1,0:T(8,128)(2,1)} %convert_element_type.57.own), custom_call_target="tpu_custom_call" | custom-call | tf_op jit(solution)/shard_map/request_rows/pallas_call | solution.py:211
  31.2 1.0 constant_dynamic-slice_fusion
  32.2 0.2 copy.26
  32.4 0.2 copy.22
  32.6 0.2 eq.167
  32.8 0.0 copy-start.6
  32.8 5.5 %fusion.9 = bf16[256,8,256]{2,1,0:T(8,128)(2,1)} fusion(s32[2048]{0:T(1024)S(1)} %eq.167, f32[2048,256]{1,0:T(8,128)} %param.7), kind=kOutput, calls=%fused_computation.25 | convolution fusion | flops 2152726528 | bytes 3153920 | tf_op jit(solution)/shard_map/dot_general | solution.py:428
  38.3 0.0 copy-done.3
  38.3 0.0 copy-start.5
  38.3 0.0 copy-start
  38.3 7.4 %all-to-all-start = ((bf16[256,8,256]{2,1,0:T(8,128)(2,1)}), bf16[256,8,256]{2,1,0:T(8,128)(2,1)S(1)}, u32[]{:S(2)}, u32[]{:S(2)}) async-start(bf16[256,8,256]{2,1,0:T(8,128)(2,1)} %fusion.9), calls=%async_computation | async-start | bytes 2097152 | tf_op jit(solution)/shard_map/all_to_all | solution.py:17
  45.6 0.0 copy-done.6
  45.7 4.8 %add_convert_fusion = bf16[256,4096]{1,0:T(8,128)(2,1)S(1)} fusion(s32[256]{0:T(256)S(1)} %bitcast.48, s32[256]{0:T(256)S(1)} %bitcast.49, s32[256]{0:T(256)S(1)} %bitcast.43, s32[256]{0:T(256)S(1)} %bitcast.44, s32[256]{0:T(256)S(1)} %bitcast.45, s32[256]{0:T(256)S(1)} %bitcast.46, s32[256]{0:T(256)S(1)} %bitcast.47, s32[256]{0:T(256)S(1)} %bitcast.42), kind=kLoop, calls=%fused_computation.7 | loop fusion | flops 25165824 | bytes 2105344 | tf_op jit(solution)/shard_map/convert_element_type | solution.py:438
  50.5 0.0 copy-done.5
  50.5 0.1 copy.18
  50.6 0.1 eq.164
  50.7 0.0 copy-done
  50.7 0.8 copy.23
  51.6 0.0 copy-start.7
  51.6 25.6 %finish_gather.1 = bf16[2,4,8,2,2,16,256]{6,5,4,3,2,1,0:T(8,128)(2,1)} custom-call(bf16[4,4,16,256]{3,2,1,0:T(8,128)(2,1)} %get-tuple-element.9.plane_a, bf16[2,4,2,16,256]{4,3,2,1,0:T(8,128)(2,1)} %get-tuple-element.10.plane_b), custom_call_target="tpu_custom_call" | custom-call | tf_op jit(solution)/shard_map/finish_gather/pallas_call | solution.py:248
  77.1 3.2 %fusion.22 = f32[256,256]{0,1:T(8,128)} fusion(bf16[256,4096]{1,0:T(8,128)(2,1)S(1)} %add_convert_fusion, bf16[4096,256]{1,0:T(8,128)(2,1)} %bitcast.37), kind=kOutput, calls=%fused_computation.45 | convolution fusion | flops 536870912 | bytes 4456448 | tf_op jit(solution)/shard_map/dot_general | solution.py:441
  80.4 0.0 all-to-all-done
  80.4 2.4 %multiply_reduce_fusion = (f32[256]{0:T(256)S(1)}, f32[256,256]{0,1:T(8,128)}) fusion(f32[256,256]{0,1:T(8,128)} %copy.23, f32[256,256]{0,1:T(8,128)} %fusion.22, bf16[256,8,256]{2,1,0:T(8,128)(2,1)S(1)} %all-to-all-done, s32[2048]{0:T(1024)S(1)} %eq.164), kind=kOutput, calls=%fused_computation.37 | convolution fusion | flops 269156096 | bytes 1844224 | tf_op jit(solution)/shard_map/dot_general | solution.py:442
  82.8 0.0 copy-done.7
  82.8 1.8 %fusion.8 = bf16[256,8,256]{2,1,0:T(8,128)(2,1)} fusion(s32[2048]{0:T(1024)S(1)} %eq.164, f32[256,256]{1,0:T(8,128)S(1)} %copy-done, f32[256]{0:T(256)S(1)} %divide_subtract_fusion), kind=kOutput, calls=%fused_computation.24 | convolution fusion | flops 269680640 | bytes 1319936 | tf_op jit(solution)/shard_map/dot_general | solution.py:449
  84.6 7.8 %all-to-all-start.1 = ((bf16[256,8,256]{2,1,0:T(8,128)(2,1)}), bf16[256,8,256]{2,1,0:T(8,128)(2,1)S(1)}, u32[]{:S(2)}, u32[]{:S(2)}) async-start(bf16[256,8,256]{2,1,0:T(8,128)(2,1)} %fusion.8), calls=%async_computation.1 | async-start | bytes 2097152 | tf_op jit(solution)/shard_map/all_to_all | solution.py:17
  92.4 0.8 fusion.20
  93.3 2.9 %convolution_add_fusion = f32[4096,256]{1,0:T(8,128)} fusion(f32[4096,256]{1,0:T(8,128)S(1)} %fusion.20, bf16[256,4096]{1,0:T(8,128)(2,1)S(1)} %add_convert_fusion, f32[256,256]{1,0:T(8,128)S(1)} %copy-done, f32[256]{0:T(256)S(1)} %divide_subtract_fusion), kind=kOutput, calls=%fused_computation.6 | convolution fusion | flops 538181632 | bytes 10748928 | tf_op jit(solution)/shard_map/dot_general | solution.py:453
  96.2 0.0 copy-start.2
  96.2 57.6 %update_hot.1 = (f32[16,256]{1,0:T(8,128)}, bf16[2,4,8,2,2,16,256]{6,5,4,3,2,1,0:T(8,128)(2,1)}) custom-call(f32[2,4,8,2,2,16,256]{6,5,4,3,2,1,0:T(8,128)} %bitcast.36, f32[16,256]{1,0:T(8,128)} %copy-done.3), custom_call_target="tpu_custom_call" | custom-call | tf_op jit(solution)/shard_map/update_hot/pallas_call | solution.py:382
  153.8 0.0 copy-done.2
  153.8 0.8 copy.24
  154.6 3.9 %bitcast_convert_fusion = f32[4096,256]{1,0:T(8,128)} fusion(bf16[2,4,8,2,2,16,256]{6,5,4,3,2,1,0:T(8,128)(2,1)} %get-tuple-element.12), kind=kLoop, calls=%fused_computation.21 | loop fusion | flops 1048576 | bytes 6291456 | tf_op jit(solution)/shard_map/convert_element_type | solution.py:462
  158.5 0.0 copy-start.1
  158.5 0.0 copy-start.4
  158.5 0.0 copy-start.8
  158.5 0.0 all-to-all-done.1
  158.6 4.9 %fusion = f32[2048,256]{1,0:T(8,128)S(1)} fusion(s32[2048]{0:T(1024)S(1)} %eq.167, bf16[256,8,256]{2,1,0:T(8,128)(2,1)S(1)} %all-to-all-done.1), kind=kOutput, calls=%fused_computation.2 | convolution fusion | flops 2151677952 | bytes 3153920 | tf_op jit(solution)/shard_map/dot_general | solution.py:456
  163.5 0.0 copy-done.1
  163.5 0.0 copy-done.4
  163.5 0.0 copy-done.8
  163.5 2.4 %fusion.5 = f32[2048,256]{1,0:T(8,128)} fusion(f32[2048,256]{1,0:T(8,128)S(1)} %copy-done.1, f32[2048,256]{1,0:T(8,128)S(1)} %fusion, f32[16,256]{1,0:T(8,128)S(1)} %copy-done.4, s32[16]{0:T(128)S(1)} %copy-done.8), kind=kOutput, calls=%fused_computation.18 | convolution fusion | flops 102268928 | bytes 6307904 | tf_op jit(solution)/shard_map/dot_general | solution.py:458
  (4 shorter events, 0.1 us)
Async XLA Ops:
  3.5 34.8 %copy-start.3 = (f32[16,256]{1,0:T(8,128)}, f32[16,256]{1,0:T(8,128)S(1)}, u32[]{:S(2)}) copy-start(f32[16,256]{1,0:T(8,128)S(1)} %gather_fusion) | copy-start | bytes 49156
  32.8 12.9 %copy-start.6 = (s32[256,8]{0,1:T(8,128)S(1)}, s32[256,8]{0,1:T(8,128)}, u32[]{:S(2)}) copy-start(s32[256,8]{0,1:T(8,128)} %param.11) | copy-start | bytes 24580
  38.3 12.2 %copy-start.5 = (s32[1,256,8]{1,2,0:T(8,128)S(1)}, s32[1,256,8]{1,2,0:T(8,128)}, u32[]{:S(2)}) copy-start(s32[1,256,8]{1,2,0:T(8,128)} %param.10) | copy-start | bytes 24580
  38.3 12.5 %copy-start = (f32[256,256]{1,0:T(8,128)S(1)}, f32[256,256]{1,0:T(8,128)}, u32[]{:S(2)}) copy-start(f32[256,256]{1,0:T(8,128)} %param.12) | copy-start | bytes 786436
  38.3 42.1 %all-to-all-start = ((bf16[256,8,256]{2,1,0:T(8,128)(2,1)}), bf16[256,8,256]{2,1,0:T(8,128)(2,1)S(1)}, u32[]{:S(2)}, u32[]{:S(2)}) async-start(bf16[256,8,256]{2,1,0:T(8,128)(2,1)} %fusion.9), calls=%async_computation | async-start | bytes 2097152 | tf_op jit(solution)/shard_map/all_to_all | solution.py:17
  51.6 31.2 %copy-start.7 = (s32[256]{0:T(256)S(1)}, s32[256]{0:T(256)}, u32[]{:S(2)}) copy-start(s32[256]{0:T(256)} %param.13) | copy-start | bytes 3076
  84.6 74.0 %all-to-all-start.1 = ((bf16[256,8,256]{2,1,0:T(8,128)(2,1)}), bf16[256,8,256]{2,1,0:T(8,128)(2,1)S(1)}, u32[]{:S(2)}, u32[]{:S(2)}) async-start(bf16[256,8,256]{2,1,0:T(8,128)(2,1)} %fusion.8), calls=%async_computation.1 | async-start | bytes 2097152 | tf_op jit(solution)/shard_map/all_to_all | solution.py:17
  96.2 57.6 %copy-start.2 = (f32[256,256]{0,1:T(8,128)S(1)}, f32[256,256]{0,1:T(8,128)}, u32[]{:S(2)}) copy-start(f32[256,256]{0,1:T(8,128)} %get-tuple-element.31) | copy-start | bytes 786436
  158.5 5.0 %copy-start.1 = (f32[2048,256]{1,0:T(8,128)S(1)}, f32[2048,256]{1,0:T(8,128)}, u32[]{:S(2)}) copy-start(f32[2048,256]{1,0:T(8,128)} %param.7) | copy-start | bytes 6291460
  158.5 5.0 %copy-start.4 = (f32[16,256]{1,0:T(8,128)S(1)}, f32[16,256]{1,0:T(8,128)}, u32[]{:S(2)}) copy-start(f32[16,256]{1,0:T(8,128)} %get-tuple-element.11) | copy-start | bytes 49156
  158.5 5.0 %copy-start.8 = (s32[16]{0:T(128)S(1)}, s32[16]{0:T(128)}, u32[]{:S(2)}) copy-start(s32[16]{0:T(128)} %param.8) | copy-start | bytes 196

commit v4 on v3

--- a/solution.py
+++ b/solution.py
@@ -110,7 +110,7 @@
     yield
 
 
-def spread_planes(me, plane_a, plane_b, full, sender, near):
+def spread_planes(me, plane_a, plane_b, full, sender, near, meanwhile=tuple):
     n_x, n_y, n_z = me.n
     n_lo = me.dims[3]
     half = n_z // 2
@@ -131,6 +131,7 @@
     keep = [near.start(plane_a, of_x(me.x)), near.start(plane_b, of_y(me.y))]
     arrivals = [(copy, of_x((me.x + n_x - k) % n_x)) for k, copy in enumerate(over_x, 1)]
     arrivals += [(copy, of_y((me.y + n_y - k) % n_y)) for k, copy in enumerate(over_y, 1)]
+    result = meanwhile()
     for copy, landed in arrivals:
         copy.wait_recv()
         side.append(sender.start(landed, landed, me.partner()))
@@ -138,6 +139,7 @@
         copy.wait()
     for copy in side:
         copy.wait_recv()
+    return result
 
 
 class Near:
@@ -151,16 +153,20 @@
         return copy
 
 
-SEMS = [pltpu.SemaphoreType.DMA((64,)), pltpu.SemaphoreType.DMA((64,)), pltpu.SemaphoreType.DMA((8,))]
+SEMS = [pltpu.SemaphoreType.DMA((96,)), pltpu.SemaphoreType.DMA((96,)), pltpu.SemaphoreType.DMA((16,))]
 IN_VMEM = pl.BlockSpec(memory_space=pltpu.VMEM)
 
 
 def request_kernel(
-    dims, width, asks, own, got, plane_a, plane_b, from_z, from_y, line,
+    dims, width, asks, table, slot, pick, got, plane_a, plane_b, old, counts,
+    from_z, from_y, line, own,
     send_sem, recv_sem, near_sem,
 ):
     me = Place(dims)
     n_x, n_y, n_z = me.n
+    for i in range(old.shape[0]):
+        old[pl.ds(i, 1), :] = table[pl.ds(slot[i], 1), :]
+    own[...] = old[...].astype(own.dtype)
     me.meet()
     sender, near = Sender(send_sem, recv_sem), Near(near_sem)
 
@@ -171,6 +177,16 @@
         stage.append(sender.start(asks.at[z], from_z.at[me.z], device))
     lines = spread_lines(me, own, line, plane_a, plane_b, sender, near)
     next(lines)
+
+    def count(i, carry):
+        ids = i * 64 + lax.broadcasted_iota(jnp.int32, (64, pick.shape[1]), 0)
+        total = jnp.zeros(ids.shape, jnp.float32)
+        for j in range(pick.shape[0]):
+            total = total + jnp.where(ids == pick[pl.ds(j, 1), :], 1.0, 0.0)
+        counts[pl.ds(pl.multiple_of(i * 64, 64), 64), :] = total.astype(counts.dtype)
+        return carry
+
+    lax.fori_loop(0, counts.shape[0] // 64, count, 0)
     keep.wait()
     for copy in stage:
         copy.wait_recv()
@@ -200,39 +216,43 @@
     sender.finish()
 
 
-def request_rows(rows, own, dims):
+def request_rows(rows, table, slot, pick, dims):
     n_hi, n_y, n_z, n_lo, n_core = dims
     n_x, half = n_hi * n_lo, n_z // 2
     cap = rows.shape[1]
     width = n_x * n_core * cap
     tiles = -(-n_y * width // 128)
+    tile = (slot.shape[0], table.shape[1])
+    bf16 = jnp.bfloat16
     asks = rows.reshape(*dims, cap).transpose(2, 1, 0, 3, 4, 5).reshape(n_z, n_y * width)
     asks = jnp.pad(asks, ((0, 0), (0, tiles * 128 - n_y * width)))
-    got, plane_a, plane_b = pl.pallas_call(
+    got, plane_a, plane_b, old, counts = pl.pallas_call(
         functools.partial(request_kernel, dims, width),
         out_shape=(
             jax.ShapeDtypeStruct((n_core, n_x, n_y, n_z, 1, 128), jnp.int32),
-            jax.ShapeDtypeStruct((n_y, half, *own.shape), own.dtype),
-            jax.ShapeDtypeStruct((n_hi, half, n_lo, *own.shape), own.dtype),
+            jax.ShapeDtypeStruct((n_y, half, *tile), bf16),
+            jax.ShapeDtypeStruct((n_hi, half, n_lo, *tile), bf16),
+            jax.ShapeDtypeStruct(tile, jnp.float32),
+            jax.ShapeDtypeStruct((math.prod(dims) * tile[0], pick.shape[0]), bf16),
         ),
-        in_specs=[IN_VMEM] * 2,
-        out_specs=(IN_VMEM,) * 3,
+        in_specs=[IN_VMEM, IN_VMEM, pl.BlockSpec(memory_space=pltpu.SMEM), IN_VMEM],
+        out_specs=(IN_VMEM,) * 5,
         scratch_shapes=[
             pltpu.VMEM((n_z, tiles, 1, 128), jnp.int32),
             pltpu.VMEM((n_y, n_z, 1, 128), jnp.int32),
-            pltpu.VMEM((n_z, *own.shape), own.dtype),
+            pltpu.VMEM((n_z, *tile), bf16),
+            pltpu.VMEM(tile, bf16),
             *SEMS,
         ],
         compiler_params=pltpu.CompilerParams(collective_id=0, has_side_effects=True),
         name="request_rows",
-    )(asks.reshape(n_z, tiles, 1, 128), own)
+    )(asks.reshape(n_z, tiles, 1, 128), table, slot, pick.T)
     r, g = lax.axis_index("rows"), lax.axis_index("grp")
     y = lax.rem(lax.div(r, n_z), n_y)
     pair = lax.div(r, n_y * n_z) * (n_lo * n_core) + g
     lane = lax.rem(y * width, 128) + pair * cap
     got = lax.dynamic_slice_in_dim(got.reshape(-1, 128), lane, cap, axis=1)
-    got = got.reshape(n_core, n_hi, n_lo, n_y, n_z, cap).transpose(1, 3, 4, 2, 0, 5)
-    return got.reshape(-1), plane_a, plane_b
+    return got.reshape(n_core, n_hi, n_lo, n_y, n_z, cap), plane_a, plane_b, old, counts
 
 
 def finish_kernel(dims, plane_a, plane_b, full, send_sem, recv_sem, near_sem):
@@ -258,7 +278,8 @@
 
 
 def update_kernel(
-    dims, part, old, grad, full,
+    dims, part, old, slots, grad, full, cold,
+    cold_z, cold_ya, cold_xa, cold_xb, cold_yb,
     twin_a, twin_b, packed_a, packed_b, in_a, in_b, in_a2, in_b2,
     line, in_z, fresh, spread, plane_a, plane_b,
     send_sem, recv_sem, near_sem,
@@ -271,6 +292,12 @@
     me.meet()
     sender, near = Sender(send_sem, recv_sem), Near(near_sem)
     f32, bf16 = jnp.float32, jnp.bfloat16
+
+    keep_cold = near.start(slots.at[:, :, me.z], cold_z.at[me.z])
+    cold_stage = []
+    for k in range(1, n_z):
+        z, device = me.along_z(k)
+        cold_stage.append(sender.start(slots.at[:, :, z], cold_z.at[me.z], device))
 
     chunks = []
     for k in [*range(1, max(n_x, n_y)), 0]:
@@ -360,6 +387,26 @@
     for k in range(1, n_z):
         z, device = me.along_z(k)
         stage.append(sender.start(line.at[z], in_z.at[k - 1], device))
+
+    keep_cold.wait()
+    for copy in cold_stage:
+        copy.wait_recv()
+
+    def ya(y):
+        return cold_z.at[low, :, y]
+
+    def xb(x):
+        return cold_z.at[top, x // n_lo, :, x % n_lo]
+
+    keep_cold = [near.start(ya(me.y), cold_ya.at[me.y]), near.start(xb(me.x), cold_xb.at[me.x])]
+    cold_stage = []
+    for k in range(1, n_y):
+        y, device = me.along_y(k)
+        cold_stage.append(sender.start(ya(y), cold_ya.at[me.y], device))
+    for k in range(1, n_x):
+        x, device = me.along_x(k)
+        cold_stage.append(sender.start(xb(x), cold_xb.at[me.x], device))
+
     for copy in stage:
         copy.wait_recv()
     total = line[me.z]
@@ -368,26 +415,72 @@
     grad[...] = total
     fresh[...] = (old[...] - 0.1 * total).astype(bf16)
 
-    for _ in spread_lines(me, fresh, spread, plane_a, plane_b, sender, near):
-        pass
-    spread_planes(me, plane_a, plane_b, full, sender, near)
+    lines = spread_lines(me, fresh, spread, plane_a, plane_b, sender, near)
+    next(lines)
+
+    for copy in keep_cold:
+        copy.wait()
+    for copy in cold_stage:
+        copy.wait_recv()
+
+    def xa(x):
+        return cold_ya.at[:, :, x // n_lo, x % n_lo]
+
+    def yb(y):
+        return cold_xb.at[:, :, y]
+
+    keep_cold = [near.start(xa(me.x), cold_xa.at[me.x]), near.start(yb(me.y), cold_yb.at[:, me.y])]
+    cold_stage = []
+    for k in range(1, n_x):
+        x, device = me.along_x(k)
+        cold_stage.append(sender.start(xa(x), cold_xa.at[me.x], device))
+    for k in range(1, n_y):
+        y, device = me.along_y(k)
+        cold_stage.append(sender.start(yb(y), cold_yb.at[:, me.y], device))
+
+    next(lines)
+    next(lines)
+
+    def swap_cold():
+        for copy in keep_cold:
+            copy.wait()
+        for copy in cold_stage:
+            copy.wait_recv()
+        pairs = [(cold_xa, cold.at[me.c, :, :, low]), (cold_yb, cold.at[me.c, :, :, top])]
+        kept = [near.start(src.at[:, :, :, me.c], dst) for src, dst in pairs]
+        sent = [sender.start(src.at[:, :, :, 1 - me.c], dst, me.partner()) for src, dst in pairs]
+        return kept, sent
+
+    kept, sent = spread_planes(me, plane_a, plane_b, full, sender, near, swap_cold)
+    for copy in kept:
+        copy.wait()
+    for copy in sent:
+        copy.wait_recv()
     sender.finish()
 
 
-def update_hot(part, old, dims):
+def update_hot(part, old, slots, dims):
     n_hi, n_y, n_z, n_lo, _ = dims
     n_x, half = n_hi * n_lo, n_z // 2
     tile = old.shape
     f32, bf16 = jnp.float32, jnp.bfloat16
-    grad, full = pl.pallas_call(
+    unit = slots.shape[-2:]
+    n_core = dims[4]
+    grad, full, cold = pl.pallas_call(
         functools.partial(update_kernel, dims),
         out_shape=(
             jax.ShapeDtypeStruct(tile, f32),
             jax.ShapeDtypeStruct((*dims, *tile), bf16),
+            jax.ShapeDtypeStruct((n_core, n_x, n_y, n_z, *unit), bf16),
         ),
-        in_specs=[IN_VMEM] * 2,
-        out_specs=(IN_VMEM,) * 2,
+        in_specs=[IN_VMEM] * 3,
+        out_specs=(IN_VMEM,) * 3,
         scratch_shapes=[
+            pltpu.VMEM((n_z, n_hi, n_y, n_lo, n_core, *unit), bf16),
+            pltpu.VMEM((n_y, half, n_hi, n_lo, n_core, *unit), bf16),
+            pltpu.VMEM((n_x, n_y, half, n_core, *unit), bf16),
+            pltpu.VMEM((n_x, half, n_y, n_core, *unit), bf16),
+            pltpu.VMEM((n_x, n_y, half, n_core, *unit), bf16),
             pltpu.VMEM((n_x, n_y, half, *tile), f32),
             pltpu.VMEM((n_y, n_hi, half, n_lo, *tile), f32),
             pltpu.VMEM((n_x - 1, n_y, half, *tile), bf16),
@@ -406,22 +499,24 @@
         ],
         compiler_params=pltpu.CompilerParams(collective_id=1, has_side_effects=True),
         name="update_hot",
-    )(part.reshape(*dims, *tile), old)
-    return grad, full.reshape(-1, tile[1])
+    )(part.reshape(*dims, *tile), old, slots.reshape(*dims, *unit))
+    return grad, full.reshape(-1, tile[1]), cold.reshape(-1, unit[1])
 
 
 def body(dims, table, hot_slot, cold_row, cold_bag, hot_pick, dense, label):
     n = math.prod(dims)
     n_table, width = table.shape
     samples = dense.shape[0]
-    own_hot = hot_slot.shape[0]
     cap = cold_row.shape[2]
     slots = cold_row.shape[1] * cap
     f32, bf16 = jnp.float32, jnp.bfloat16
     rounded = table.astype(bf16)
 
-    hot_old = table[hot_slot]
-    arrived, plane_a, plane_b = request_rows(cold_row[0], hot_old.astype(bf16), dims)
+    asked, plane_a, plane_b, hot_old, counts = request_rows(
+        cold_row[0], table, hot_slot, hot_pick, dims
+    )
+    arrived = asked.transpose(1, 3, 4, 2, 0, 5).reshape(slots)
+    asked = asked.reshape(slots)
 
     row_ids = jnp.arange(n_table, dtype=jnp.int32)
     at_row = (arrived[:, None] == row_ids[None, :]).astype(bf16)
@@ -431,29 +526,24 @@
     bags = cold_bag[0].reshape(slots)
     sample_ids = jnp.arange(samples, dtype=jnp.int32)
     selector = (sample_ids[:, None] == bags[None, :]).astype(bf16)
-    hot_ids = jnp.arange(n * own_hot, dtype=jnp.int32)
-    counts = sum(
-        (hot_pick[:, j][:, None] == hot_ids[None, :]).astype(f32)
-        for j in range(hot_pick.shape[1])
-    ).astype(bf16)
-    counts = lax.optimization_barrier(counts)
     hot_copy = finish_gather(plane_a, plane_b, dims)
-    hot_pooled = jnp.dot(counts, hot_copy, preferred_element_type=f32)
+    first = (((0,), (0,)), ((), ()))
+    hot_pooled = lax.dot_general(counts, hot_copy, first, preferred_element_type=f32)
     pooled = jnp.dot(selector, returned, preferred_element_type=f32) + hot_pooled
     score = jnp.sum(pooled * dense, axis=1) / width**0.5
     err = jax.nn.sigmoid(score) - label.astype(f32)
     grad = err[:, None] * dense
     high, low = split_bf16(grad)
 
-    first = (((0,), (0,)), ((), ()))
     slot_grad = lax.dot_general(selector, high, first, preferred_element_type=f32).astype(bf16)
-    delivered = exchange(slot_grad.reshape(n, cap, width)).reshape(slots, width)
-
-    hot_local = lax.dot_general(counts, high, first, preferred_element_type=f32)
-    hot_local = hot_local + lax.dot_general(counts, low, first, preferred_element_type=f32)
-    own_grad, hot_new = update_hot(hot_local, hot_old, dims)
-
-    table_grad = lax.dot_general(at_row, delivered, first, preferred_element_type=f32)
+    hot_local = jnp.dot(counts, high, preferred_element_type=f32)
+    hot_local = hot_local + jnp.dot(counts, low, preferred_element_type=f32)
+    own_grad, hot_new, delivered = update_hot(
+        hot_local, hot_old, slot_grad.reshape(n, cap, width), dims
+    )
+
+    from_row = (row_ids[:, None] == asked[None, :]).astype(bf16)
+    table_grad = jnp.dot(from_row, delivered, preferred_element_type=f32)
     at_hot = (row_ids[:, None] == hot_slot[None, :]).astype(f32)
     table_grad = table_grad + jnp.dot(
         at_hot, own_grad, precision=lax.Precision.HIGHEST, preferred_element_type=f32

time: 166 us -> 157 us (0.946)
  starting transfers between devices: 15.2 us -> 7.23 us
  other arithmetic: 10 us -> 4.03 us
  Pallas kernels: 109 us -> 114 us
  local copies, waits for them, and re-layouts: 7.31 us -> 5.39 us
    all_to_all x2 -> x1, starting transfers between devices: 15.2 us -> 7.23 us  [exchange(): return lax.all_to_all(blocks, AXES, split_axis=0, concat_axis=0, tiled=True)]
    convert_element_type x2 -> x0, other arithmetic: 5.41 us -> none  [the longest x1 4.81 us: body(): counts = sum(((hot_pick[:, j][:, None] == hot_ids[None, :]).astype(f32) f...]
    pallas_call x1, Pallas kernels: 25.4 us -> 27.9 us  [request_rows(): pl.pallas_call(functools.partial(request_kernel, dims, width), out_shape=...]
    dot_general x4, matrix products: 11.9 us -> 14.2 us  [the longest x1 4.99 us: body(): hot_local = hot_local + jnp.dot(counts, low, preferred_element_type=f32)]
    pallas_call x1, Pallas kernels: 57.6 us -> 59.8 us  [update_hot(): pl.pallas_call(functools.partial(update_kernel, dims), out_shape=(jax.Sha...]
    gather x1 -> x0, local copies, waits for them, and re-layouts: 2.16 us -> none  [body(): hot_old = table[hot_slot]]
  transfers between devices with their start and end apart: 2 -> 1, of which waited for: 0 -> 0; matrix products, arithmetic and copies ran while one was open for 11% -> 3% of each run, Pallas kernels for 50% -> 17%
where the time goes in v4:
time: 157 us; the launch traced here: 156 us
  Pallas kernels  114 us (73%)
  matrix products  24.7 us (16%)
  starting transfers between devices  7.23 us (5%)
  local copies, waits for them, and re-layouts  5.39 us (3%)
  other arithmetic  4.03 us (3%)
    pallas_call x1, Pallas kernels, update_hot(): pl.pallas_call(functools.partial(update_kernel, dims), out_shape=(jax.Sha...  59.8 us
    pallas_call x1, Pallas kernels, request_rows(): pl.pallas_call(functools.partial(request_kernel, dims, width), out_shape=...  27.9 us
    pallas_call x1, Pallas kernels, finish_gather(): pl.pallas_call(functools.partial(finish_kernel, dims), out_shape=jax.Shap...  26.4 us
    all_to_all x1, starting transfers between devices, exchange(): return lax.all_to_all(blocks, AXES, split_axis=0, concat_axis=0, tiled=True)  7.23 us
    dot_general x1, matrix products, body(): hot_local = hot_local + jnp.dot(counts, low, preferred_element_type=f32)  4.99 us
    convert_element_type x1, other arithmetic, body(): return (pooled, new_table, hot_new.astype(f32))  4.02 us
    dot_general x1, matrix products, body(): looked = jnp.dot(at_row, rounded, preferred_element_type=f32).astype(bf16)  3.96 us
    dot_general x1, matrix products, body(): lax.dot_general(counts, hot_copy, first, preferred_element_type=f32)  3.22 us
  transfers between devices with their start and end apart: 1, of which 0 were waited for; matrix products, arithmetic and copies ran while one was open for 3% of the time, Pallas kernels for 17%

profile of v4, /device:TPU:1, one launch (start us, length us, event | category | flops | bytes accessed | tf_op | source)
XLA Modules:
  0.0 156.3 jit_solution(7350448934798467471)
XLA Ops:
  0.6 0.0 copy-start.1
  0.7 1.0 copy.19
  1.7 0.8 reshape.40.asks
  2.5 27.9 %request_rows.1 = (s32[2,4,4,8,1,128]{5,4,3,2,1,0:T(1,128)}, bf16[4,4,16,256]{3,2,1,0:T(8,128)(2,1)}, bf16[2,4,2,16,256]{4,3,2,1,0:T(8,128)(2,1)}, f32[16,256]{1,0:T(8,128)}, bf16[4096,256]{1,0:T(8,128)(2,1)}) custom-call(s32[8,2,1,128]{3,2,1,0:T(1,128)} %reshape.40.asks, f32[2048,256]{1,0:T(8,128)} %table.1, s32[16]{0:T(128)} %slot.1, s32[8,256]{1,0:T(8,128)} %bitcast.34), custom_call_target="tpu_custom_call" | custom-call | tf_op jit(solution)/shard_map/request_rows/pallas_call | solution.py:229
  30.4 1.0 constant_dynamic-slice_fusion
  31.4 0.2 copy.25
  31.6 0.2 copy.22
  31.8 0.2 eq.62
  32.0 0.0 copy-done.1
  32.0 4.0 %fusion.8 = bf16[256,8,256]{2,1,0:T(8,128)(2,1)} fusion(s32[2048]{0:T(1024)S(1)} %eq.62, f32[2048,256]{1,0:T(8,128)S(1)} %copy-done.1), kind=kOutput, calls=%fused_computation.15 | convolution fusion | flops 2152726528 | bytes 3153920 | tf_op jit(solution)/shard_map/dot_general | solution.py:523
  35.9 0.0 copy-start.6
  35.9 0.0 copy-start.3
  35.9 7.2 %all-to-all-start = ((bf16[256,8,256]{2,1,0:T(8,128)(2,1)}), bf16[256,8,256]{2,1,0:T(8,128)(2,1)S(1)}, u32[]{:S(2)}, u32[]{:S(2)}) async-start(bf16[256,8,256]{2,1,0:T(8,128)(2,1)} %fusion.8), calls=%async_computation | async-start | bytes 2097152 | tf_op jit(solution)/shard_map/all_to_all | solution.py:17
  43.2 0.0 copy-start
  43.2 0.1 eq.67
  43.3 0.0 copy-done.6
  43.3 0.1 copy.18
  43.4 0.1 eq.59
  43.5 0.0 copy-done.3
  43.6 0.8 copy.23
  44.4 26.4 %finish_gather.1 = bf16[2,4,8,2,2,16,256]{6,5,4,3,2,1,0:T(8,128)(2,1)} custom-call(bf16[4,4,16,256]{3,2,1,0:T(8,128)(2,1)} %get-tuple-element.13.plane_a, bf16[2,4,2,16,256]{4,3,2,1,0:T(8,128)(2,1)} %get-tuple-element.14.plane_b), custom_call_target="tpu_custom_call" | custom-call | tf_op jit(solution)/shard_map/finish_gather/pallas_call | solution.py:268
  70.8 0.0 copy-done
  70.8 3.2 %fusion.19 = f32[256,256]{0,1:T(8,128)} fusion(bf16[4096,256]{1,0:T(8,128)(2,1)S(1)} %copy-done, bf16[4096,256]{1,0:T(8,128)(2,1)} %bitcast.28), kind=kOutput, calls=%fused_computation.31 | convolution fusion | flops 536870912 | bytes 4456448 | tf_op jit(solution)/shard_map/dot_general | solution.py:531
  74.0 0.0 copy-start.8
  74.0 0.0 all-to-all-done
  74.0 2.4 %multiply_reduce_fusion = (f32[256]{0:T(256)S(1)}, f32[256,256]{0,1:T(8,128)}) fusion(f32[256,256]{0,1:T(8,128)} %copy.23, f32[256,256]{0,1:T(8,128)} %fusion.19, bf16[256,8,256]{2,1,0:T(8,128)(2,1)S(1)} %all-to-all-done, s32[2048]{0:T(1024)S(1)} %eq.59), kind=kOutput, calls=%fused_computation.26 | convolution fusion | flops 269156096 | bytes 1844224 | tf_op jit(solution)/shard_map/dot_general | solution.py:532
  76.5 0.0 copy-done.8
  76.5 1.8 %convolution_convert_fusion = bf16[2048,256]{1,0:T(8,128)(2,1)} fusion(s32[2048]{0:T(1024)S(1)} %eq.59, f32[256,256]{1,0:T(8,128)S(1)} %copy-done.3, f32[256]{0:T(256)S(1)} %divide_subtract_fusion), kind=kOutput, calls=%fused_computation.11 | convolution fusion | flops 269680640 | bytes 1319936 | tf_op jit(solution)/shard_map/dot_general | solution.py:538
  78.3 0.0 copy-start.4
  78.3 2.8 %fusion.18 = f32[4096,256]{1,0:T(8,128)} fusion(bf16[4096,256]{1,0:T(8,128)(2,1)S(1)} %copy-done, f32[256,256]{1,0:T(8,128)S(1)} %copy-done.3, f32[256]{0:T(256)S(1)} %divide_subtract_fusion), kind=kOutput, calls=%fused_computation.30 | convolution fusion | flops 537067520 | bytes 6554624 | tf_op jit(solution)/shard_map/dot_general | solution.py:539
  81.1 0.0 copy-done.4
  81.1 0.8 copy.24
  81.9 5.0 %convolution_add_fusion = f32[4096,256]{1,0:T(8,128)} fusion(f32[4096,256]{1,0:T(8,128)} %fusion.18, bf16[4096,256]{1,0:T(8,128)(2,1)S(1)} %copy-done, f32[256,256]{1,0:T(8,128)S(1)} %copy-done.3, f32[256]{0:T(256)S(1)} %divide_subtract_fusion), kind=kOutput, calls=%fused_computation.6 | convolution fusion | flops 538181632 | bytes 10748928 | tf_op jit(solution)/shard_map/dot_general | solution.py:540
  86.9 59.8 %update_hot.1 = (f32[16,256]{1,0:T(8,128)}, bf16[2,4,8,2,2,16,256]{6,5,4,3,2,1,0:T(8,128)(2,1)}, bf16[2,4,4,8,8,256]{5,4,3,2,1,0:T(8,128)(2,1)}) custom-call(f32[2,4,8,2,2,16,256]{6,5,4,3,2,1,0:T(8,128)} %bitcast.27, f32[16,256]{1,0:T(8,128)} %get-tuple-element.15.old, bf16[2,4,8,2,2,8,256]{6,5,4,3,2,1,0:T(8,128)(2,1)} %bitcast.30), custom_call_target="tpu_custom_call" | custom-call | tf_op jit(solution)/shard_map/update_hot/pallas_call | solution.py:469
  146.7 0.0 copy-start.9
  146.7 4.0 %bitcast_convert_fusion = f32[4096,256]{1,0:T(8,128)} fusion(bf16[2,4,8,2,2,16,256]{6,5,4,3,2,1,0:T(8,128)(2,1)} %get-tuple-element.18), kind=kLoop, calls=%fused_computation.12 | loop fusion | flops 1048576 | bytes 6291456 | tf_op jit(solution)/shard_map/convert_element_type | solution.py:552
  150.7 0.0 copy-done.9
  150.7 0.0 copy-start.2
  150.7 0.0 copy-start.5
  150.7 0.0 copy-start.7
  150.7 3.2 %fusion.1 = f32[2048,256]{1,0:T(8,128)S(1)} fusion(bf16[2048,256]{1,0:T(8,128)(2,1)S(1)} %bitcast.35, s32[2048]{0:T(1024)S(1)} %eq.67), kind=kOutput, calls=%fused_computation.3 | convolution fusion | flops 2151677952 | bytes 3153920 | tf_op jit(solution)/shard_map/dot_general | solution.py:546
  153.9 0.0 copy-done.2
  154.0 0.0 copy-done.5
  154.0 0.0 copy-done.7
  154.0 2.3 %fusion.5 = f32[2048,256]{1,0:T(8,128)} fusion(f32[2048,256]{1,0:T(8,128)S(1)} %copy-done.2, f32[2048,256]{1,0:T(8,128)S(1)} %fusion.1, f32[16,256]{1,0:T(8,128)S(1)} %copy-done.5, s32[16]{0:T(128)S(1)} %copy-done.7), kind=kOutput, calls=%fused_computation.9 | convolution fusion | flops 102268928 | bytes 6307904 | tf_op jit(solution)/shard_map/dot_general | solution.py:548
  (2 shorter events, 0.0 us)
Async XLA Ops:
  0.6 31.3 %copy-start.1 = (f32[2048,256]{1,0:T(8,128)S(1)}, f32[2048,256]{1,0:T(8,128)}, u32[]{:S(2)}) copy-start(f32[2048,256]{1,0:T(8,128)} %table.1) | copy-start | bytes 6291460
  35.9 7.4 %copy-start.6 = (s32[1,256,8]{1,2,0:T(8,128)S(1)}, s32[1,256,8]{1,2,0:T(8,128)}, u32[]{:S(2)}) copy-start(s32[1,256,8]{1,2,0:T(8,128)} %param.10) | copy-start | bytes 24580
  35.9 7.6 %copy-start.3 = (f32[256,256]{1,0:T(8,128)S(1)}, f32[256,256]{1,0:T(8,128)}, u32[]{:S(2)}) copy-start(f32[256,256]{1,0:T(8,128)} %param.12) | copy-start | bytes 786436
  35.9 38.1 %all-to-all-start = ((bf16[256,8,256]{2,1,0:T(8,128)(2,1)}), bf16[256,8,256]{2,1,0:T(8,128)(2,1)S(1)}, u32[]{:S(2)}, u32[]{:S(2)}) async-start(bf16[256,8,256]{2,1,0:T(8,128)(2,1)} %fusion.8), calls=%async_computation | async-start | bytes 2097152 | tf_op jit(solution)/shard_map/all_to_all | solution.py:17
  43.2 27.6 %copy-start = (bf16[4096,256]{1,0:T(8,128)(2,1)S(1)}, bf16[4096,256]{1,0:T(8,128)(2,1)}, u32[]{:S(2)}) copy-start(bf16[4096,256]{1,0:T(8,128)(2,1)} %get-tuple-element.12) | copy-start | bytes 6291460
  74.0 2.5 %copy-start.8 = (s32[256]{0:T(256)S(1)}, s32[256]{0:T(256)}, u32[]{:S(2)}) copy-start(s32[256]{0:T(256)} %param.13) | copy-start | bytes 3076
  78.3 2.8 %copy-start.4 = (f32[256,256]{0,1:T(8,128)S(1)}, f32[256,256]{0,1:T(8,128)}, u32[]{:S(2)}) copy-start(f32[256,256]{0,1:T(8,128)} %get-tuple-element.29) | copy-start | bytes 786436
  146.7 4.0 %copy-start.9 = (bf16[2,4,4,8,8,256]{5,4,3,2,1,0:T(8,128)(2,1)S(1)}, bf16[2,4,4,8,8,256]{5,4,3,2,1,0:T(8,128)(2,1)}, u32[]{:S(2)}) copy-start(bf16[2,4,4,8,8,256]{5,4,3,2,1,0:T(8,128)(2,1)} %get-tuple-element.16) | copy-start | bytes 3145732
  150.7 3.2 %copy-start.2 = (f32[2048,256]{1,0:T(8,128)S(1)}, f32[2048,256]{1,0:T(8,128)}, u32[]{:S(2)}) copy-start(f32[2048,256]{1,0:T(8,128)} %table.1) | copy-start | bytes 6291460
  150.7 3.3 %copy-start.5 = (f32[16,256]{1,0:T(8,128)S(1)}, f32[16,256]{1,0:T(8,128)}, u32[]{:S(2)}) copy-start(f32[16,256]{1,0:T(8,128)} %get-tuple-element.17) | copy-start | bytes 49156
  150.7 3.3 %copy-start.7 = (s32[16]{0:T(128)S(1)}, s32[16]{0:T(128)}, u32[]{:S(2)}) copy-start(s32[16]{0:T(128)} %slot.1) | copy-start | bytes 196

commit v5 on v4

--- a/solution.py
+++ b/solution.py
@@ -51,16 +51,19 @@
     def partner(self):
         return self.device(self.x, self.y, self.z, 1 - self.c)
 
-    def meet(self):
-        barrier = pltpu.get_barrier_semaphore()
+    def greet(self):
         n_x, n_y, n_z = self.n
         peers = [self.along_z(k)[1] for k in range(1, n_z)]
         peers += [self.along_y(k)[1] for k in range(1, n_y)]
         peers += [self.along_x(k)[1] for k in range(1, n_x)]
         peers += [self.partner()]
         for peer in peers:
-            pl.semaphore_signal(barrier, inc=1, device_id=peer, device_id_type=MESH)
-        pl.semaphore_wait(barrier, len(peers))
+            pl.semaphore_signal(
+                pltpu.get_barrier_semaphore(), inc=1, device_id=peer, device_id_type=MESH
+            )
+
+    def meet(self):
+        pl.semaphore_wait(pltpu.get_barrier_semaphore(), sum(self.n) - 2)
 
 
 class Sender:
@@ -153,7 +156,11 @@
         return copy
 
 
-SEMS = [pltpu.SemaphoreType.DMA((96,)), pltpu.SemaphoreType.DMA((96,)), pltpu.SemaphoreType.DMA((16,))]
+def semaphores(remote, near):
+    dma = pltpu.SemaphoreType.DMA
+    return [dma((remote,)), dma((remote,)), dma((near,))]
+
+
 IN_VMEM = pl.BlockSpec(memory_space=pltpu.VMEM)
 
 
@@ -164,9 +171,21 @@
 ):
     me = Place(dims)
     n_x, n_y, n_z = me.n
+    me.greet()
     for i in range(old.shape[0]):
         old[pl.ds(i, 1), :] = table[pl.ds(slot[i], 1), :]
     own[...] = old[...].astype(own.dtype)
+
+    def count(i, carry):
+        ids = i * 64 + lax.broadcasted_iota(jnp.int32, (64, pick.shape[1]), 0)
+        total = jnp.zeros(ids.shape, jnp.float32)
+        for j in range(pick.shape[0]):
+            total = total + jnp.where(ids == pick[pl.ds(j, 1), :], 1.0, 0.0)
+        counts[pl.ds(pl.multiple_of(i * 64, 64), 64), :] = total.astype(counts.dtype)
+        return carry
+
+    pieces = counts.shape[0] // 64
+    lax.fori_loop(0, pieces // 4, count, 0)
     me.meet()
     sender, near = Sender(send_sem, recv_sem), Near(near_sem)
 
@@ -178,15 +197,7 @@
     lines = spread_lines(me, own, line, plane_a, plane_b, sender, near)
     next(lines)
 
-    def count(i, carry):
-        ids = i * 64 + lax.broadcasted_iota(jnp.int32, (64, pick.shape[1]), 0)
-        total = jnp.zeros(ids.shape, jnp.float32)
-        for j in range(pick.shape[0]):
-            total = total + jnp.where(ids == pick[pl.ds(j, 1), :], 1.0, 0.0)
-        counts[pl.ds(pl.multiple_of(i * 64, 64), 64), :] = total.astype(counts.dtype)
-        return carry
-
-    lax.fori_loop(0, counts.shape[0] // 64, count, 0)
+    lax.fori_loop(pieces // 4, pieces, count, 0)
     keep.wait()
     for copy in stage:
         copy.wait_recv()
@@ -242,7 +253,7 @@
             pltpu.VMEM((n_y, n_z, 1, 128), jnp.int32),
             pltpu.VMEM((n_z, *tile), bf16),
             pltpu.VMEM(tile, bf16),
-            *SEMS,
+            *semaphores(2 * (n_x + n_y + n_z) - 5, 6),
         ],
         compiler_params=pltpu.CompilerParams(collective_id=0, has_side_effects=True),
         name="request_rows",
@@ -257,6 +268,7 @@
 
 def finish_kernel(dims, plane_a, plane_b, full, send_sem, recv_sem, near_sem):
     me = Place(dims)
+    me.greet()
     me.meet()
     sender, near = Sender(send_sem, recv_sem), Near(near_sem)
     spread_planes(me, plane_a, plane_b, full, sender, near)
@@ -264,13 +276,14 @@
 
 
 def finish_gather(plane_a, plane_b, dims):
+    n_x, n_y = dims[0] * dims[3], dims[1]
     tile = plane_a.shape[-2:]
     full = pl.pallas_call(
         functools.partial(finish_kernel, dims),
         out_shape=jax.ShapeDtypeStruct((*dims, *tile), plane_a.dtype),
         in_specs=[IN_VMEM] * 2,
         out_specs=IN_VMEM,
-        scratch_shapes=SEMS,
+        scratch_shapes=semaphores(2 * (n_x + n_y) - 2, 2),
         compiler_params=pltpu.CompilerParams(collective_id=2, has_side_effects=True),
         name="finish_gather",
     )(plane_a, plane_b)
@@ -278,7 +291,8 @@
 
 
 def update_kernel(
-    dims, part, old, slots, grad, full, cold,
+    dims, counts, high, rest, old, slots, grad, full, cold,
+    part,
     cold_z, cold_ya, cold_xa, cold_xb, cold_yb,
     twin_a, twin_b, packed_a, packed_b, in_a, in_b, in_a2, in_b2,
     line, in_z, fresh, spread, plane_a, plane_b,
@@ -289,9 +303,23 @@
     n_x = n_hi * n_lo
     half = n_z // 2
     low, top = pl.ds(0, half), pl.ds(half, half)
+    f32, bf16 = jnp.float32, jnp.bfloat16
+    me.greet()
+
+    rows = counts.shape[0] // (n_hi * n_y * 2)
+
+    def multiply(i, carry):
+        some = counts[pl.ds(pl.multiple_of(i * rows, rows), rows), :]
+        total = jnp.dot(some, high[...], preferred_element_type=f32)
+        total = total + jnp.dot(some, rest[...], preferred_element_type=f32)
+        x_hi, y, z = i // (2 * n_y), i // 2 % n_y, i % 2 * half
+        shape = (half, *part.shape[3:])
+        part[x_hi, y, pl.ds(z, half)] = total.reshape(shape)
+        return carry
+
+    lax.fori_loop(0, n_hi * n_y * 2, multiply, 0)
     me.meet()
     sender, near = Sender(send_sem, recv_sem), Near(near_sem)
-    f32, bf16 = jnp.float32, jnp.bfloat16
 
     keep_cold = near.start(slots.at[:, :, me.z], cold_z.at[me.z])
     cold_stage = []
@@ -388,6 +416,17 @@
         z, device = me.along_z(k)
         stage.append(sender.start(line.at[z], in_z.at[k - 1], device))
 
+    for copy in stage:
+        copy.wait_recv()
+    total = line[me.z]
+    for k in range(n_z - 1):
+        total = total + in_z[k]
+    grad[...] = total
+    fresh[...] = (old[...] - 0.1 * total).astype(bf16)
+
+    lines = spread_lines(me, fresh, spread, plane_a, plane_b, sender, near)
+    next(lines)
+
     keep_cold.wait()
     for copy in cold_stage:
         copy.wait_recv()
@@ -407,59 +446,47 @@
         x, device = me.along_x(k)
         cold_stage.append(sender.start(xb(x), cold_xb.at[me.x], device))
 
-    for copy in stage:
-        copy.wait_recv()
-    total = line[me.z]
-    for k in range(n_z - 1):
-        total = total + in_z[k]
-    grad[...] = total
-    fresh[...] = (old[...] - 0.1 * total).astype(bf16)
-
-    lines = spread_lines(me, fresh, spread, plane_a, plane_b, sender, near)
-    next(lines)
-
-    for copy in keep_cold:
-        copy.wait()
-    for copy in cold_stage:
-        copy.wait_recv()
-
-    def xa(x):
-        return cold_ya.at[:, :, x // n_lo, x % n_lo]
-
-    def yb(y):
-        return cold_xb.at[:, :, y]
-
-    keep_cold = [near.start(xa(me.x), cold_xa.at[me.x]), near.start(yb(me.y), cold_yb.at[:, me.y])]
-    cold_stage = []
-    for k in range(1, n_x):
-        x, device = me.along_x(k)
-        cold_stage.append(sender.start(xa(x), cold_xa.at[me.x], device))
-    for k in range(1, n_y):
-        y, device = me.along_y(k)
-        cold_stage.append(sender.start(yb(y), cold_yb.at[:, me.y], device))
-
     next(lines)
     next(lines)
 
-    def swap_cold():
+    def turn_cold():
         for copy in keep_cold:
             copy.wait()
         for copy in cold_stage:
             copy.wait_recv()
-        pairs = [(cold_xa, cold.at[me.c, :, :, low]), (cold_yb, cold.at[me.c, :, :, top])]
-        kept = [near.start(src.at[:, :, :, me.c], dst) for src, dst in pairs]
-        sent = [sender.start(src.at[:, :, :, 1 - me.c], dst, me.partner()) for src, dst in pairs]
+
+        def xa(x):
+            return cold_ya.at[:, :, x // n_lo, x % n_lo]
+
+        def yb(y):
+            return cold_xb.at[:, :, y]
+
+        kept = [near.start(xa(me.x), cold_xa.at[me.x]), near.start(yb(me.y), cold_yb.at[:, me.y])]
+        sent = []
+        for k in range(1, n_x):
+            x, device = me.along_x(k)
+            sent.append(sender.start(xa(x), cold_xa.at[me.x], device))
+        for k in range(1, n_y):
+            y, device = me.along_y(k)
+            sent.append(sender.start(yb(y), cold_yb.at[:, me.y], device))
         return kept, sent
 
-    kept, sent = spread_planes(me, plane_a, plane_b, full, sender, near, swap_cold)
+    kept, sent = spread_planes(me, plane_a, plane_b, full, sender, near, turn_cold)
     for copy in kept:
         copy.wait()
     for copy in sent:
         copy.wait_recv()
+    pairs = [(cold_xa, cold.at[me.c, :, :, low]), (cold_yb, cold.at[me.c, :, :, top])]
+    kept = [near.start(src.at[:, :, :, me.c], dst) for src, dst in pairs]
+    sent = [sender.start(src.at[:, :, :, 1 - me.c], dst, me.partner()) for src, dst in pairs]
+    for copy in kept:
+        copy.wait()
+    for copy in sent:
+        copy.wait_recv()
     sender.finish()
 
 
-def update_hot(part, old, slots, dims):
+def update_hot(counts, high, rest, old, slots, dims):
     n_hi, n_y, n_z, n_lo, _ = dims
     n_x, half = n_hi * n_lo, n_z // 2
     tile = old.shape
@@ -473,9 +500,10 @@
             jax.ShapeDtypeStruct((*dims, *tile), bf16),
             jax.ShapeDtypeStruct((n_core, n_x, n_y, n_z, *unit), bf16),
         ),
-        in_specs=[IN_VMEM] * 3,
+        in_specs=[IN_VMEM] * 5,
         out_specs=(IN_VMEM,) * 3,
         scratch_shapes=[
+            pltpu.VMEM((*dims, *tile), f32),
             pltpu.VMEM((n_z, n_hi, n_y, n_lo, n_core, *unit), bf16),
             pltpu.VMEM((n_y, half, n_hi, n_lo, n_core, *unit), bf16),
             pltpu.VMEM((n_x, n_y, half, n_core, *unit), bf16),
@@ -495,11 +523,11 @@
             pltpu.VMEM((n_z, *tile), bf16),
             pltpu.VMEM((n_y, half, *tile), bf16),
             pltpu.VMEM((n_hi, half, n_lo, *tile), bf16),
-            *SEMS,
+            *semaphores(8 * (n_x + n_y) + 3 * n_z - 13, 12),
         ],
         compiler_params=pltpu.CompilerParams(collective_id=1, has_side_effects=True),
         name="update_hot",
-    )(part.reshape(*dims, *tile), old, slots.reshape(*dims, *unit))
+    )(counts, high, rest, old, slots.reshape(*dims, *unit))
     return grad, full.reshape(-1, tile[1]), cold.reshape(-1, unit[1])
 
 
@@ -533,13 +561,11 @@
     score = jnp.sum(pooled * dense, axis=1) / width**0.5
     err = jax.nn.sigmoid(score) - label.astype(f32)
     grad = err[:, None] * dense
-    high, low = split_bf16(grad)
+    high, rest = split_bf16(grad)
 
     slot_grad = lax.dot_general(selector, high, first, preferred_element_type=f32).astype(bf16)
-    hot_local = jnp.dot(counts, high, preferred_element_type=f32)
-    hot_local = hot_local + jnp.dot(counts, low, preferred_element_type=f32)
     own_grad, hot_new, delivered = update_hot(
-        hot_local, hot_old, slot_grad.reshape(n, cap, width), dims
+        counts, high, rest, hot_old, slot_grad.reshape(n, cap, width), dims
     )
 
     from_row = (row_ids[:, None] == asked[None, :]).astype(bf16)

time: 157 us -> 151 us (0.962)
  matrix products: 24.7 us -> 17.6 us
    dot_general x2 -> x0, matrix products: 7.78 us -> none  [the longest x1 4.99 us: body(): hot_local = hot_local + jnp.dot(counts, low, preferred_element_type=f32)]
    pallas_call x1, Pallas kernels: 59.8 us -> 61.6 us  [update_hot(): pl.pallas_call(functools.partial(update_kernel, dims), out_shape=(jax.Sha...]
    pallas_call x1, Pallas kernels: 26.4 us -> 24.8 us  [finish_gather(): pl.pallas_call(functools.partial(finish_kernel, dims), out_shape=jax.Shap...]
    unnamed x24 -> x20, local copies, waits for them, and re-layouts: 2.8 us -> 3.78 us
  transfers between devices with their start and end apart: 1 -> 1, of which waited for: 0 -> 1; matrix products, arithmetic and copies ran while one was open for 3% -> 3% of each run, Pallas kernels for 17% -> 16%
where the time goes in v5:
time: 151 us
  Pallas kernels  113 us (75%)
  matrix products  17.6 us (12%)
  starting transfers between devices  7.36 us (5%)
  local copies, waits for them, and re-layouts  6.38 us (4%)
  other arithmetic  4.8 us (3%)
    pallas_call x1, Pallas kernels, update_hot(): pl.pallas_call(functools.partial(update_kernel, dims), out_shape=(jax.Sha...  61.6 us
    pallas_call x1, Pallas kernels, request_rows(): pl.pallas_call(functools.partial(request_kernel, dims, width), out_shape=...  26.5 us
    pallas_call x1, Pallas kernels, finish_gather(): pl.pallas_call(functools.partial(finish_kernel, dims), out_shape=jax.Shap...  24.8 us
    all_to_all x1, starting transfers between devices, exchange(): return lax.all_to_all(blocks, AXES, split_axis=0, concat_axis=0, tiled=True)  7.36 us
    convert_element_type x1, other arithmetic, body(): return (pooled, new_table, hot_new.astype(f32))  4.02 us
    dot_general x1, matrix products, body(): looked = jnp.dot(at_row, rounded, preferred_element_type=f32).astype(bf16)  3.96 us
    dot_general x1, matrix products, body(): lax.dot_general(counts, hot_copy, first, preferred_element_type=f32)  3.86 us
    unnamed x20, local copies, waits for them, and re-layouts  3.78 us
  transfers between devices with their start and end apart: 1, of which 1 were waited for; matrix products, arithmetic and copies ran while one was open for 3% of the time, Pallas kernels for 16%

profile of v5, /device:TPU:1, one launch (start us, length us, event | category | flops | bytes accessed | tf_op | source)
XLA Modules:
  0.0 150.5 jit_solution(12885178912549248946)
XLA Ops:
  0.6 0.0 copy-start
  0.7 1.0 copy.19
  1.7 0.8 reshape.37.asks
  2.5 26.5 %request_rows.1 = (s32[2,4,4,8,1,128]{5,4,3,2,1,0:T(1,128)}, bf16[4,4,16,256]{3,2,1,0:T(8,128)(2,1)}, bf16[2,4,2,16,256]{4,3,2,1,0:T(8,128)(2,1)}, f32[16,256]{1,0:T(8,128)}, bf16[4096,256]{1,0:T(8,128)(2,1)}) custom-call(s32[8,2,1,128]{3,2,1,0:T(1,128)} %reshape.37.asks, f32[2048,256]{1,0:T(8,128)} %table.1, s32[16]{0:T(128)} %slot.1, s32[8,256]{1,0:T(8,128)} %bitcast.31), custom_call_target="tpu_custom_call" | custom-call | tf_op jit(solution)/shard_map/request_rows/pallas_call | solution.py:240
  29.0 1.0 constant_dynamic-slice_fusion
  30.0 0.2 copy.25
  30.1 0.2 copy.22
  30.3 0.2 eq.62
  30.5 0.0 copy-done
  30.5 4.0 %fusion.8 = bf16[256,8,256]{2,1,0:T(8,128)(2,1)} fusion(s32[2048]{0:T(1024)S(1)} %eq.62, f32[2048,256]{1,0:T(8,128)S(1)} %copy-done), kind=kOutput, calls=%fused_computation.14 | convolution fusion | flops 2152726528 | bytes 3153920 | tf_op jit(solution)/shard_map/dot_general | solution.py:551
  34.5 0.0 copy-start.4
  34.5 0.0 copy-start.1
  34.5 7.4 %all-to-all-start = ((bf16[256,8,256]{2,1,0:T(8,128)(2,1)}), bf16[256,8,256]{2,1,0:T(8,128)(2,1)S(1)}, u32[]{:S(2)}, u32[]{:S(2)}) async-start(bf16[256,8,256]{2,1,0:T(8,128)(2,1)} %fusion.8), calls=%async_computation | async-start | bytes 2097152 | tf_op jit(solution)/shard_map/all_to_all | solution.py:17
  41.8 0.1 eq.67
  42.0 0.0 copy-done.4
  42.0 0.1 copy.18
  42.1 0.1 eq.59
  42.2 0.0 copy-done.1
  42.2 0.8 copy.23
  43.1 24.8 %finish_gather.1 = bf16[2,4,8,2,2,16,256]{6,5,4,3,2,1,0:T(8,128)(2,1)} custom-call(bf16[4,4,16,256]{3,2,1,0:T(8,128)(2,1)} %get-tuple-element.13.plane_a, bf16[2,4,2,16,256]{4,3,2,1,0:T(8,128)(2,1)} %get-tuple-element.14.plane_b), custom_call_target="tpu_custom_call" | custom-call | tf_op jit(solution)/shard_map/finish_gather/pallas_call | solution.py:281
  67.9 3.9 %fusion.16 = f32[256,256]{0,1:T(8,128)} fusion(bf16[4096,256]{1,0:T(8,128)(2,1)} %get-tuple-element.12.counts, bf16[4096,256]{1,0:T(8,128)(2,1)} %bitcast.25), kind=kOutput, calls=%fused_computation.28 | convolution fusion | flops 536870912 | bytes 4456448 | tf_op jit(solution)/shard_map/dot_general | solution.py:559
  71.7 0.0 copy-start.6
  71.7 0.8 all-to-all-done
  72.5 2.4 %multiply_reduce_fusion = (f32[256]{0:T(256)S(1)}, f32[256,256]{0,1:T(8,128)}) fusion(f32[256,256]{0,1:T(8,128)} %copy.23, f32[256,256]{0,1:T(8,128)} %fusion.16, bf16[256,8,256]{2,1,0:T(8,128)(2,1)S(1)} %all-to-all-done, s32[2048]{0:T(1024)S(1)} %eq.59), kind=kOutput, calls=%fused_computation.25 | convolution fusion | flops 269156096 | bytes 1844224 | tf_op jit(solution)/shard_map/dot_general | solution.py:560
  74.9 0.0 copy-done.6
  75.0 0.8 fusion.15
  75.7 0.0 copy-start.2
  75.7 1.8 %copy.24 = f32[256,256]{1,0:T(8,128)} copy(f32[256,256]{0,1:T(8,128)} %get-tuple-element.31) | data formatting | bytes 524288
  77.6 1.7 %convolution_convert_fusion = bf16[2048,256]{1,0:T(8,128)(2,1)} fusion(bf16[256,256]{1,0:T(8,128)(2,1)S(1)} %get-tuple-element.29.high, s32[2048]{0:T(1024)S(1)} %eq.59), kind=kOutput, calls=%fused_computation.10 | convolution fusion | flops 269484032 | bytes 1187840 | tf_op jit(solution)/shard_map/dot_general | solution.py:566
  79.3 0.0 copy-done.2
  79.3 61.6 %update_hot.1 = (f32[16,256]{1,0:T(8,128)}, bf16[2,4,8,2,2,16,256]{6,5,4,3,2,1,0:T(8,128)(2,1)}, bf16[2,4,4,8,8,256]{5,4,3,2,1,0:T(8,128)(2,1)}) custom-call(bf16[4096,256]{1,0:T(8,128)(2,1)} %get-tuple-element.12.counts, bf16[256,256]{1,0:T(8,128)(2,1)} %copy-done.2, bf16[256,256]{1,0:T(8,128)(2,1)} %get-tuple-element.28.rest, ...), custom_call_target="tpu_custom_call" | custom-call | tf_op jit(solution)/shard_map/update_hot/pallas_call | solution.py:496
  140.8 0.0 copy-start.7
  140.8 4.0 %bitcast_convert_fusion = f32[4096,256]{1,0:T(8,128)} fusion(bf16[2,4,8,2,2,16,256]{6,5,4,3,2,1,0:T(8,128)(2,1)} %get-tuple-element.18), kind=kLoop, calls=%fused_computation.11 | loop fusion | flops 1048576 | bytes 6291456 | tf_op jit(solution)/shard_map/convert_element_type | solution.py:578
  144.9 0.0 copy-done.7
  144.9 0.0 copy-start.3
  144.9 0.0 copy-start.5
  144.9 3.2 %fusion.1 = f32[2048,256]{1,0:T(8,128)S(1)} fusion(bf16[2048,256]{1,0:T(8,128)(2,1)S(1)} %bitcast.32, s32[2048]{0:T(1024)S(1)} %eq.67), kind=kOutput, calls=%fused_computation.3 | convolution fusion | flops 2151677952 | bytes 3153920 | tf_op jit(solution)/shard_map/dot_general | solution.py:572
  148.1 0.0 copy-done.3
  148.1 0.0 copy-done.5
  148.1 2.4 %fusion.5 = f32[2048,256]{1,0:T(8,128)} fusion(f32[2048,256]{1,0:T(8,128)S(1)} %copy-done, f32[2048,256]{1,0:T(8,128)S(1)} %fusion.1, f32[16,256]{1,0:T(8,128)S(1)} %copy-done.3, s32[16]{0:T(128)S(1)} %copy-done.5), kind=kOutput, calls=%fused_computation.8 | convolution fusion | flops 102268928 | bytes 6307904 | tf_op jit(solution)/shard_map/dot_general | solution.py:574
  (2 shorter events, 0.0 us)
Async XLA Ops:
  0.6 29.9 %copy-start = (f32[2048,256]{1,0:T(8,128)S(1)}, f32[2048,256]{1,0:T(8,128)}, u32[]{:S(2)}) copy-start(f32[2048,256]{1,0:T(8,128)} %table.1) | copy-start | bytes 6291460
  34.5 7.5 %copy-start.4 = (s32[1,256,8]{1,2,0:T(8,128)S(1)}, s32[1,256,8]{1,2,0:T(8,128)}, u32[]{:S(2)}) copy-start(s32[1,256,8]{1,2,0:T(8,128)} %param.10) | copy-start | bytes 24580
  34.5 7.7 %copy-start.1 = (f32[256,256]{1,0:T(8,128)S(1)}, f32[256,256]{1,0:T(8,128)}, u32[]{:S(2)}) copy-start(f32[256,256]{1,0:T(8,128)} %param.12) | copy-start | bytes 786436
  34.5 38.0 %all-to-all-start = ((bf16[256,8,256]{2,1,0:T(8,128)(2,1)}), bf16[256,8,256]{2,1,0:T(8,128)(2,1)S(1)}, u32[]{:S(2)}, u32[]{:S(2)}) async-start(bf16[256,8,256]{2,1,0:T(8,128)(2,1)} %fusion.8), calls=%async_computation | async-start | bytes 2097152 | tf_op jit(solution)/shard_map/all_to_all | solution.py:17
  71.7 3.2 %copy-start.6 = (s32[256]{0:T(256)S(1)}, s32[256]{0:T(256)}, u32[]{:S(2)}) copy-start(s32[256]{0:T(256)} %param.13) | copy-start | bytes 3076
  75.7 3.5 %copy-start.2 = (bf16[256,256]{1,0:T(8,128)(2,1)}, bf16[256,256]{1,0:T(8,128)(2,1)S(1)}, u32[]{:S(2)}) copy-start(bf16[256,256]{1,0:T(8,128)(2,1)S(1)} %get-tuple-element.29.high) | copy-start | bytes 393220
  140.8 4.0 %copy-start.7 = (bf16[2,4,4,8,8,256]{5,4,3,2,1,0:T(8,128)(2,1)S(1)}, bf16[2,4,4,8,8,256]{5,4,3,2,1,0:T(8,128)(2,1)}, u32[]{:S(2)}) copy-start(bf16[2,4,4,8,8,256]{5,4,3,2,1,0:T(8,128)(2,1)} %get-tuple-element.16) | copy-start | bytes 3145732
  144.9 3.2 %copy-start.3 = (f32[16,256]{1,0:T(8,128)S(1)}, f32[16,256]{1,0:T(8,128)}, u32[]{:S(2)}) copy-start(f32[16,256]{1,0:T(8,128)} %get-tuple-element.17) | copy-start | bytes 49156
  144.9 3.2 %copy-start.5 = (s32[16]{0:T(128)S(1)}, s32[16]{0:T(128)}, u32[]{:S(2)}) copy-start(s32[16]{0:T(128)} %slot.1) | copy-start | bytes 196

commit v6 on v5

--- a/solution.py
+++ b/solution.py
@@ -321,11 +321,36 @@
     me.meet()
     sender, near = Sender(send_sem, recv_sem), Near(near_sem)
 
-    keep_cold = near.start(slots.at[:, :, me.z], cold_z.at[me.z])
-    cold_stage = []
-    for k in range(1, n_z):
+    near_first = sorted(range(1, n_z), key=lambda k: min(k, n_z - k))
+    cold_in = {0: near.start(slots.at[:, :, me.z], cold_z.at[0])}
+    for k in near_first:
         z, device = me.along_z(k)
-        cold_stage.append(sender.start(slots.at[:, :, z], cold_z.at[me.z], device))
+        cold_in[k] = sender.start(slots.at[:, :, z], cold_z.at[k], device)
+    kept, sent = [], []
+
+    def turn_cold(k):
+        if k:
+            cold_in[k].wait_recv()
+        else:
+            cold_in[k].wait()
+        if k < half:
+            for j in range(n_y):
+                y, device = me.along_y(j)
+                src, dst = cold_z.at[k, :, y], cold_ya.at[me.y, k]
+                if j:
+                    sent.append(sender.start(src, dst, device))
+                else:
+                    kept.append(near.start(src, dst))
+        else:
+            for j in range(n_x):
+                x, device = me.along_x(j)
+                src, dst = cold_z.at[k, x // n_lo, :, x % n_lo], cold_xb.at[me.x, k - half]
+                if j:
+                    sent.append(sender.start(src, dst, device))
+                else:
+                    kept.append(near.start(src, dst))
+
+    early = [0, *near_first[: n_z // 2]]
 
     chunks = []
     for k in [*range(1, max(n_x, n_y)), 0]:
@@ -395,6 +420,8 @@
         x, device = me.along_x(k)
         src = twin_b.at[0, x // n_lo, :, x % n_lo]
         stage.append(sender.start(src, in_b2.at[k - 1], device))
+    for k in early:
+        turn_cold(k)
     for copy in stage:
         copy.wait_recv()
 
@@ -415,7 +442,8 @@
     for k in range(1, n_z):
         z, device = me.along_z(k)
         stage.append(sender.start(line.at[z], in_z.at[k - 1], device))
-
+    for k in near_first[n_z // 2 :]:
+        turn_cold(k)
     for copy in stage:
         copy.wait_recv()
     total = line[me.z]
@@ -427,61 +455,46 @@
     lines = spread_lines(me, fresh, spread, plane_a, plane_b, sender, near)
     next(lines)
 
-    keep_cold.wait()
-    for copy in cold_stage:
-        copy.wait_recv()
-
-    def ya(y):
-        return cold_z.at[low, :, y]
-
-    def xb(x):
-        return cold_z.at[top, x // n_lo, :, x % n_lo]
-
-    keep_cold = [near.start(ya(me.y), cold_ya.at[me.y]), near.start(xb(me.x), cold_xb.at[me.x])]
-    cold_stage = []
-    for k in range(1, n_y):
-        y, device = me.along_y(k)
-        cold_stage.append(sender.start(ya(y), cold_ya.at[me.y], device))
-    for k in range(1, n_x):
-        x, device = me.along_x(k)
-        cold_stage.append(sender.start(xb(x), cold_xb.at[me.x], device))
-
-    next(lines)
-    next(lines)
-
-    def turn_cold():
-        for copy in keep_cold:
-            copy.wait()
-        for copy in cold_stage:
-            copy.wait_recv()
-
-        def xa(x):
-            return cold_ya.at[:, :, x // n_lo, x % n_lo]
-
-        def yb(y):
-            return cold_xb.at[:, :, y]
-
-        kept = [near.start(xa(me.x), cold_xa.at[me.x]), near.start(yb(me.y), cold_yb.at[:, me.y])]
-        sent = []
-        for k in range(1, n_x):
-            x, device = me.along_x(k)
-            sent.append(sender.start(xa(x), cold_xa.at[me.x], device))
-        for k in range(1, n_y):
-            y, device = me.along_y(k)
-            sent.append(sender.start(yb(y), cold_yb.at[:, me.y], device))
-        return kept, sent
-
-    kept, sent = spread_planes(me, plane_a, plane_b, full, sender, near, turn_cold)
     for copy in kept:
         copy.wait()
     for copy in sent:
         copy.wait_recv()
-    pairs = [(cold_xa, cold.at[me.c, :, :, low]), (cold_yb, cold.at[me.c, :, :, top])]
-    kept = [near.start(src.at[:, :, :, me.c], dst) for src, dst in pairs]
-    sent = [sender.start(src.at[:, :, :, 1 - me.c], dst, me.partner()) for src, dst in pairs]
-    for copy in kept:
+
+    def xa(x):
+        return cold_ya.at[:, :, x // n_lo, x % n_lo]
+
+    def yb(y):
+        return cold_xb.at[:, :, y]
+
+    kept = [near.start(xa(me.x), cold_xa.at[me.x]), near.start(yb(me.y), cold_yb.at[:, me.y])]
+    sent = []
+    for k in range(1, n_x):
+        x, device = me.along_x(k)
+        sent.append(sender.start(xa(x), cold_xa.at[me.x], device))
+    for k in range(1, n_y):
+        y, device = me.along_y(k)
+        sent.append(sender.start(yb(y), cold_yb.at[:, me.y], device))
+
+    next(lines)
+    next(lines)
+
+    def swap_cold():
+        for copy in kept:
+            copy.wait()
+        for copy in sent:
+            copy.wait_recv()
+        own, other = [], []
+        for k in range(n_z):
+            src = cold_xa if k < half else cold_yb
+            dst = cold.at[me.c, :, :, (me.z + n_z - k) % n_z]
+            own.append(near.start(src.at[:, :, k % half, me.c], dst))
+            other.append(sender.start(src.at[:, :, k % half, 1 - me.c], dst, me.partner()))
+        return own, other
+
+    own, other = spread_planes(me, plane_a, plane_b, full, sender, near, swap_cold)
+    for copy in own:
         copy.wait()
-    for copy in sent:
+    for copy in other:
         copy.wait_recv()
     sender.finish()
 
@@ -523,7 +536,7 @@
             pltpu.VMEM((n_z, *tile), bf16),
             pltpu.VMEM((n_y, half, *tile), bf16),
             pltpu.VMEM((n_hi, half, n_lo, *tile), bf16),
-            *semaphores(8 * (n_x + n_y) + 3 * n_z - 13, 12),
+            *semaphores((half + 7) * (n_x + n_y) + 4 * n_z - 2 * half - 13, 2 * n_z + 8),
         ],
         compiler_params=pltpu.CompilerParams(collective_id=1, has_side_effects=True),
         name="update_hot",

time: 151 us -> 146 us (0.967)
  Pallas kernels: 113 us -> 108 us
    pallas_call x1, Pallas kernels: 61.6 us -> 56.3 us  [update_hot(): pl.pallas_call(functools.partial(update_kernel, dims), out_shape=(jax.Sha...]
  transfers between devices with their start and end apart: 1 -> 1, of which waited for: 1 -> 1; matrix products, arithmetic and copies ran while one was open for 3% -> 3% of each run, Pallas kernels for 16% -> 17%
where the time goes in v6:
time: 146 us; the launch traced here: 145 us
  Pallas kernels  108 us (74%)
  matrix products  17.6 us (12%)
  starting transfers between devices  7.36 us (5%)
  local copies, waits for them, and re-layouts  6.38 us (4%)
  other arithmetic  4.8 us (3%)
    pallas_call x1, Pallas kernels, update_hot(): pl.pallas_call(functools.partial(update_kernel, dims), out_shape=(jax.Sha...  56.3 us
    pallas_call x1, Pallas kernels, request_rows(): pl.pallas_call(functools.partial(request_kernel, dims, width), out_shape=...  26.5 us
    pallas_call x1, Pallas kernels, finish_gather(): pl.pallas_call(functools.partial(finish_kernel, dims), out_shape=jax.Shap...  24.8 us
    all_to_all x1, starting transfers between devices, exchange(): return lax.all_to_all(blocks, AXES, split_axis=0, concat_axis=0, tiled=True)  7.36 us
    convert_element_type x1, other arithmetic, body(): return (pooled, new_table, hot_new.astype(f32))  4.02 us
    dot_general x1, matrix products, body(): looked = jnp.dot(at_row, rounded, preferred_element_type=f32).astype(bf16)  3.96 us
    dot_general x1, matrix products, body(): lax.dot_general(counts, hot_copy, first, preferred_element_type=f32)  3.86 us
    unnamed x20, local copies, waits for them, and re-layouts  3.78 us
  transfers between devices with their start and end apart: 1, of which 1 were waited for; matrix products, arithmetic and copies ran while one was open for 3% of the time, Pallas kernels for 17%

profile of v6, /device:TPU:1, one launch (start us, length us, event | category | flops | bytes accessed | tf_op | source)
XLA Modules:
  0.0 145.2 jit_solution(12286232213796677328)
XLA Ops:
  0.6 0.0 copy-start
  0.7 1.0 copy.19
  1.7 0.8 reshape.37.asks
  2.5 26.5 %request_rows.1 = (s32[2,4,4,8,1,128]{5,4,3,2,1,0:T(1,128)}, bf16[4,4,16,256]{3,2,1,0:T(8,128)(2,1)}, bf16[2,4,2,16,256]{4,3,2,1,0:T(8,128)(2,1)}, f32[16,256]{1,0:T(8,128)}, bf16[4096,256]{1,0:T(8,128)(2,1)}) custom-call(s32[8,2,1,128]{3,2,1,0:T(1,128)} %reshape.37.asks, f32[2048,256]{1,0:T(8,128)} %table.1, s32[16]{0:T(128)} %slot.1, s32[8,256]{1,0:T(8,128)} %bitcast.31), custom_call_target="tpu_custom_call" | custom-call | tf_op jit(solution)/shard_map/request_rows/pallas_call | solution.py:240
  29.0 1.0 constant_dynamic-slice_fusion
  30.0 0.2 copy.25
  30.1 0.2 copy.22
  30.3 0.2 eq.62
  30.5 0.0 copy-done
  30.5 4.0 %fusion.8 = bf16[256,8,256]{2,1,0:T(8,128)(2,1)} fusion(s32[2048]{0:T(1024)S(1)} %eq.62, f32[2048,256]{1,0:T(8,128)S(1)} %copy-done), kind=kOutput, calls=%fused_computation.14 | convolution fusion | flops 2152726528 | bytes 3153920 | tf_op jit(solution)/shard_map/dot_general | solution.py:564
  34.5 0.0 copy-start.4
  34.5 0.0 copy-start.1
  34.5 7.4 %all-to-all-start = ((bf16[256,8,256]{2,1,0:T(8,128)(2,1)}), bf16[256,8,256]{2,1,0:T(8,128)(2,1)S(1)}, u32[]{:S(2)}, u32[]{:S(2)}) async-start(bf16[256,8,256]{2,1,0:T(8,128)(2,1)} %fusion.8), calls=%async_computation | async-start | bytes 2097152 | tf_op jit(solution)/shard_map/all_to_all | solution.py:17
  41.8 0.1 eq.67
  42.0 0.0 copy-done.4
  42.0 0.1 copy.18
  42.1 0.1 eq.59
  42.2 0.0 copy-done.1
  42.2 0.8 copy.23
  43.1 24.8 %finish_gather.1 = bf16[2,4,8,2,2,16,256]{6,5,4,3,2,1,0:T(8,128)(2,1)} custom-call(bf16[4,4,16,256]{3,2,1,0:T(8,128)(2,1)} %get-tuple-element.13.plane_a, bf16[2,4,2,16,256]{4,3,2,1,0:T(8,128)(2,1)} %get-tuple-element.14.plane_b), custom_call_target="tpu_custom_call" | custom-call | tf_op jit(solution)/shard_map/finish_gather/pallas_call | solution.py:281
  67.9 3.9 %fusion.16 = f32[256,256]{0,1:T(8,128)} fusion(bf16[4096,256]{1,0:T(8,128)(2,1)} %get-tuple-element.12.counts, bf16[4096,256]{1,0:T(8,128)(2,1)} %bitcast.25), kind=kOutput, calls=%fused_computation.28 | convolution fusion | flops 536870912 | bytes 4456448 | tf_op jit(solution)/shard_map/dot_general | solution.py:572
  71.7 0.0 copy-start.6
  71.7 0.8 all-to-all-done
  72.5 2.4 %multiply_reduce_fusion = (f32[256]{0:T(256)S(1)}, f32[256,256]{0,1:T(8,128)}) fusion(f32[256,256]{0,1:T(8,128)} %copy.23, f32[256,256]{0,1:T(8,128)} %fusion.16, bf16[256,8,256]{2,1,0:T(8,128)(2,1)S(1)} %all-to-all-done, s32[2048]{0:T(1024)S(1)} %eq.59), kind=kOutput, calls=%fused_computation.25 | convolution fusion | flops 269156096 | bytes 1844224 | tf_op jit(solution)/shard_map/dot_general | solution.py:573
  74.9 0.0 copy-done.6
  75.0 0.8 fusion.15
  75.7 0.0 copy-start.2
  75.7 1.8 %copy.24 = f32[256,256]{1,0:T(8,128)} copy(f32[256,256]{0,1:T(8,128)} %get-tuple-element.31) | data formatting | bytes 524288
  77.6 1.7 %convolution_convert_fusion = bf16[2048,256]{1,0:T(8,128)(2,1)} fusion(bf16[256,256]{1,0:T(8,128)(2,1)S(1)} %get-tuple-element.29.high, s32[2048]{0:T(1024)S(1)} %eq.59), kind=kOutput, calls=%fused_computation.10 | convolution fusion | flops 269484032 | bytes 1187840 | tf_op jit(solution)/shard_map/dot_general | solution.py:579
  79.3 0.0 copy-done.2
  79.3 56.3 %update_hot.1 = (f32[16,256]{1,0:T(8,128)}, bf16[2,4,8,2,2,16,256]{6,5,4,3,2,1,0:T(8,128)(2,1)}, bf16[2,4,4,8,8,256]{5,4,3,2,1,0:T(8,128)(2,1)}) custom-call(bf16[4096,256]{1,0:T(8,128)(2,1)} %get-tuple-element.12.counts, bf16[256,256]{1,0:T(8,128)(2,1)} %copy-done.2, bf16[256,256]{1,0:T(8,128)(2,1)} %get-tuple-element.28.rest, ...), custom_call_target="tpu_custom_call" | custom-call | tf_op jit(solution)/shard_map/update_hot/pallas_call | solution.py:509
  135.6 0.0 copy-start.7
  135.6 4.0 %bitcast_convert_fusion = f32[4096,256]{1,0:T(8,128)} fusion(bf16[2,4,8,2,2,16,256]{6,5,4,3,2,1,0:T(8,128)(2,1)} %get-tuple-element.18), kind=kLoop, calls=%fused_computation.11 | loop fusion | flops 1048576 | bytes 6291456 | tf_op jit(solution)/shard_map/convert_element_type | solution.py:591
  139.6 0.0 copy-done.7
  139.6 0.0 copy-start.3
  139.6 0.0 copy-start.5
  139.6 3.2 %fusion.1 = f32[2048,256]{1,0:T(8,128)S(1)} fusion(bf16[2048,256]{1,0:T(8,128)(2,1)S(1)} %bitcast.32, s32[2048]{0:T(1024)S(1)} %eq.67), kind=kOutput, calls=%fused_computation.3 | convolution fusion | flops 2151677952 | bytes 3153920 | tf_op jit(solution)/shard_map/dot_general | solution.py:585
  142.8 0.0 copy-done.3
  142.8 0.0 copy-done.5
  142.8 2.4 %fusion.5 = f32[2048,256]{1,0:T(8,128)} fusion(f32[2048,256]{1,0:T(8,128)S(1)} %copy-done, f32[2048,256]{1,0:T(8,128)S(1)} %fusion.1, f32[16,256]{1,0:T(8,128)S(1)} %copy-done.3, s32[16]{0:T(128)S(1)} %copy-done.5), kind=kOutput, calls=%fused_computation.8 | convolution fusion | flops 102268928 | bytes 6307904 | tf_op jit(solution)/shard_map/dot_general | solution.py:587
  (2 shorter events, 0.0 us)
Async XLA Ops:
  0.6 29.9 %copy-start = (f32[2048,256]{1,0:T(8,128)S(1)}, f32[2048,256]{1,0:T(8,128)}, u32[]{:S(2)}) copy-start(f32[2048,256]{1,0:T(8,128)} %table.1) | copy-start | bytes 6291460
  34.5 7.5 %copy-start.4 = (s32[1,256,8]{1,2,0:T(8,128)S(1)}, s32[1,256,8]{1,2,0:T(8,128)}, u32[]{:S(2)}) copy-start(s32[1,256,8]{1,2,0:T(8,128)} %param.10) | copy-start | bytes 24580
  34.5 7.7 %copy-start.1 = (f32[256,256]{1,0:T(8,128)S(1)}, f32[256,256]{1,0:T(8,128)}, u32[]{:S(2)}) copy-start(f32[256,256]{1,0:T(8,128)} %param.12) | copy-start | bytes 786436
  34.5 38.0 %all-to-all-start = ((bf16[256,8,256]{2,1,0:T(8,128)(2,1)}), bf16[256,8,256]{2,1,0:T(8,128)(2,1)S(1)}, u32[]{:S(2)}, u32[]{:S(2)}) async-start(bf16[256,8,256]{2,1,0:T(8,128)(2,1)} %fusion.8), calls=%async_computation | async-start | bytes 2097152 | tf_op jit(solution)/shard_map/all_to_all | solution.py:17
  71.7 3.2 %copy-start.6 = (s32[256]{0:T(256)S(1)}, s32[256]{0:T(256)}, u32[]{:S(2)}) copy-start(s32[256]{0:T(256)} %param.13) | copy-start | bytes 3076
  75.7 3.5 %copy-start.2 = (bf16[256,256]{1,0:T(8,128)(2,1)}, bf16[256,256]{1,0:T(8,128)(2,1)S(1)}, u32[]{:S(2)}) copy-start(bf16[256,256]{1,0:T(8,128)(2,1)S(1)} %get-tuple-element.29.high) | copy-start | bytes 393220
  135.6 4.0 %copy-start.7 = (bf16[2,4,4,8,8,256]{5,4,3,2,1,0:T(8,128)(2,1)S(1)}, bf16[2,4,4,8,8,256]{5,4,3,2,1,0:T(8,128)(2,1)}, u32[]{:S(2)}) copy-start(bf16[2,4,4,8,8,256]{5,4,3,2,1,0:T(8,128)(2,1)} %get-tuple-element.16) | copy-start | bytes 3145732
  139.6 3.2 %copy-start.3 = (f32[16,256]{1,0:T(8,128)S(1)}, f32[16,256]{1,0:T(8,128)}, u32[]{:S(2)}) copy-start(f32[16,256]{1,0:T(8,128)} %get-tuple-element.17) | copy-start | bytes 49156
  139.6 3.2 %copy-start.5 = (s32[16]{0:T(128)S(1)}, s32[16]{0:T(128)}, u32[]{:S(2)}) copy-start(s32[16]{0:T(128)} %slot.1) | copy-start | bytes 196
